TPU v7x, 32 devices: a whole 2x2x4 slice. The times are simulated.
32 devices in a mesh: grp: 4 (over y, core), seq: 8 (over z, x).
Axes of the slice: x: 2, y: 2, z: 4, core: 2. Of those that a mesh axis runs over, the one named last changes fastest.
Arguments:
- queries: bfloat16 [16384, 512], P(('grp', 'seq')), may hold values from -8 to 8
- keys: bfloat16 [16384, 512], P(('grp', 'seq')), may hold values from -4.5 to 4.5
- values: bfloat16 [16384, 512], P(('grp', 'seq')), may hold values from -6 to 6
- resid: bfloat16 [16384, 1024], P(('grp', 'seq')), may hold values from -54 to 54
- w_out: bfloat16 [512, 1024], replicated, may hold values from -2 to 2
- block_lang: int32 [256], P(('grp', 'seq')), may hold values from 0 to 11, as said below
- w_down: bfloat16 [12, 1024, 384], P('grp', 'seq'), may hold values from -0.1875 to 0.1875
- w_up: bfloat16 [12, 384, 1024], P('grp', None, 'seq'), may hold values from -0.3125 to 0.3125
- bias_down: bfloat16 [12, 384], P('grp'), may hold values from -4 to 4
- cotangent: bfloat16 [16384, 1024], P(('grp', 'seq')), may hold values from -6 to 6
Outputs:
- grad_down: float32 [1024, 12, 384], P('seq', 'grp')
Inputs may be any that keep to these rules, and one draw needn't show every extreme that they name: Block b holds tokens b * 64 to (b + 1) * 64 - 1, and its language's owner group is block_lang[b] // 3. Of the 8 blocks of one device (blocks d * 8 to (d + 1) * 8 - 1), at most 2 have the same owner group; for every index along seq, some owner group has a block from the device of that index in every group.
All inputs are finite; a program needn't handle non-finite values.
Results may differ from a plain program's by a relative error of at most 0.022.
Values may be sent and summed in bfloat16 or wider, within the bound.
No kernel may reach another device: no remote copies, remote signals or barrier semaphores. Data moves between devices by JAX's collectives and lax.ppermute only.
A program may use at most 128 MiB of HBM per device.

v0:
```python
import functools
import math

import jax
import jax.numpy as jnp
from jax import lax
from jax.experimental import pallas as pl
from jax.experimental.pallas import tpu as pltpu
from jax.sharding import PartitionSpec as P


HD = 64
WINDOW = 256
EPSILON = 1e-05
TILE = 128
LANES = 128
MARK = 16
NEG = -1e30


VMEM = pl.BlockSpec(memory_space=pltpu.VMEM)
SMEM = pl.BlockSpec(memory_space=pltpu.SMEM)


def ring_order(size):
    return list(range(0, size, 2)) + [i for i in range(size - 1, 0, -1) if i % 2]


def ring_pairs(size, step):
    order = ring_order(size)
    return [(order[i], order[(i + step) % size]) for i in range(size)]


def ring_place(index, size):
    half = index // 2
    return jnp.where(index % 2 == 0, half, size - 1 - half)


def ring_member(place, size):
    ups = (size + 1) // 2
    return jnp.where(place < ups, 2 * place, 2 * (size - place) - 1)


def peer_of(index, step, size):
    if size & (size - 1) == 0:
        return index ^ step
    return (index + step) % size


def dot(a, b, dims):
    return lax.dot_general(a, b, (dims, ((), ())), preferred_element_type=jnp.float32)


def attend(q_ref, k_win, v_win, ctx_ref, row0, bias):
    width = q_ref.shape[1]
    group = min(width, 256)
    heads = group // HD
    for col0 in range(0, width, group):
        q_part = q_ref[row0 : row0 + TILE, col0 : col0 + group] * jnp.bfloat16(HD**-0.5)
        lane_head = lax.broadcasted_iota(jnp.int32, q_part.shape, 1) // HD
        q_diag = jnp.concatenate(
            [jnp.where(lane_head == h, q_part, jnp.zeros_like(q_part)) for h in range(heads)], axis=0
        )
        keys = k_win[:, col0 : col0 + group]
        vals = v_win[:, col0 : col0 + group]
        scores = dot(q_diag, keys, ((1,), (1,)))
        scores = scores.reshape(heads, TILE, scores.shape[1]) + bias[None]
        top = jnp.max(scores, axis=-1, keepdims=True)
        weights = jnp.exp(scores - top)
        total = jnp.sum(weights, axis=-1, keepdims=True)
        soft = (weights / total).astype(jnp.bfloat16).reshape(heads * TILE, -1)
        mixed = dot(soft, vals, ((1,), (0,)))
        picked = jnp.zeros((TILE, group), jnp.float32)
        for h in range(heads):
            picked = jnp.where(lane_head == h, mixed[h * TILE : (h + 1) * TILE], picked)
        ctx_ref[row0 : row0 + TILE, col0 : col0 + group] = picked.astype(jnp.bfloat16)


def window_bias():
    shape = (TILE, TILE + WINDOW)
    row = lax.broadcasted_iota(jnp.int32, shape, 0)
    col = lax.broadcasted_iota(jnp.int32, shape, 1)
    allowed = (col <= row + WINDOW) & (col > row)
    return jnp.where(allowed, 0.0, NEG).astype(jnp.float32), col


def finish_rows(ctx_ref, r_ref, wo_ref):
    hidden = (
        r_ref[...].astype(jnp.float32) + dot(ctx_ref[...], wo_ref[...], ((1,), (0,)))
    ).astype(jnp.bfloat16).astype(jnp.float32)
    center = hidden - jnp.mean(hidden, axis=-1, keepdims=True)
    spread = jnp.mean(center * center, axis=-1, keepdims=True)
    return (center * lax.rsqrt(spread + EPSILON)).astype(jnp.bfloat16)


def late_kernel(q_ref, k_ref, v_ref, r_ref, wo_ref, out_ref, ctx_ref):
    bias, _ = window_bias()
    for row0 in range(0, q_ref.shape[0], TILE):
        span = slice(row0, row0 + TILE + WINDOW)
        attend(q_ref, k_ref[span, :], v_ref[span, :], ctx_ref, row0, bias)
    out_ref[...] = finish_rows(ctx_ref, r_ref, wo_ref)


def block_for(lang_ref, owner, rank, lang_grp):
    block, local, seen = jnp.int32(0), jnp.int32(-1), jnp.int32(0)
    for b in range(lang_ref.shape[0]):
        lang = lang_ref[b]
        mine = lang // lang_grp == owner
        take = mine & (seen == rank)
        block = jnp.where(take, b, block)
        local = jnp.where(take, lang - owner * lang_grp, local)
        seen = seen + mine.astype(jnp.int32)
    return block, local


def early_kernel(
    groups, lang_grp, lang_ref, q_ref, rim_ref, k_ref, v_ref, r_ref, wo_ref, late_ref, *rest
):
    outs, (ctx_ref, kk_ref, vv_ref, rows_ref) = rest[:groups], rest[groups:]
    rows = q_ref.shape[0]
    width = q_ref.shape[1]
    kk_ref[:WINDOW, :] = rim_ref[:, :width]
    vv_ref[:WINDOW, :] = rim_ref[:, width:]
    kk_ref[WINDOW:, :] = k_ref[...]
    vv_ref[WINDOW:, :] = v_ref[...]
    bias, col = window_bias()
    first = lax.axis_index("seq") == 0
    for row0 in range(0, rows, TILE):
        span = slice(row0, row0 + TILE + WINDOW)
        shut = jnp.logical_and(first, col + row0 < WINDOW)
        attend(q_ref, kk_ref[span, :], vv_ref[span, :], ctx_ref, row0, jnp.where(shut, NEG, bias))
    blocks = lang_ref.shape[0]
    length = rows_ref.shape[1]
    done = finish_rows(ctx_ref, r_ref, wo_ref)
    split = rows // length
    rows_ref[:split] = done.reshape(split, length, -1)
    rows_ref[split:] = late_ref[...].reshape(blocks - split, length, -1)
    me = lax.axis_index("grp")
    for step, out_ref in enumerate(outs):
        owner = peer_of(me, step, groups)
        for j in range(out_ref.shape[0] // length):
            block, _ = block_for(lang_ref, owner, j, lang_grp)
            out_ref[j * length : (j + 1) * length, :] = rows_ref[block]


def pack_kernel(groups, lang_grp, lang_ref, c_ref, *outs):
    length = c_ref.shape[1]
    me = lax.axis_index("grp")
    for step, out_ref in enumerate(outs):
        owner = peer_of(me, step, groups)
        cap = (out_ref.shape[0] - MARK) // length
        row = lax.broadcasted_iota(jnp.int32, (MARK, out_ref.shape[1]), 0)
        mark = jnp.full(row.shape, -1.0, jnp.float32)
        for j in range(cap):
            block, local = block_for(lang_ref, owner, j, lang_grp)
            out_ref[j * length : (j + 1) * length, :] = c_ref[block]
            mark = jnp.where(row == j, local.astype(jnp.float32), mark)
        out_ref[cap * length :, :] = mark.astype(jnp.bfloat16)


def gelu_slope(v):
    rate = math.sqrt(2 / math.pi)
    square = v * v
    t = jnp.tanh(rate * v * (1.0 + 0.044715 * square))
    return 0.5 * (1.0 + t) + (0.5 * rate) * v * (1.0 - t * t) * (1.0 + (3 * 0.044715) * square)


def project(x, cot, downs, ups, marks, length, lang_grp):
    pre, back = [], []
    for l in range(lang_grp):
        w_down = jnp.concatenate([d[l] for d in downs], axis=0)
        w_up = jnp.concatenate([u[l] for u in ups], axis=1)
        pre.append(dot(x, w_down, ((1,), (0,))))
        back.append(dot(cot, w_up, ((1,), (1,))))
    for j, lang in enumerate(marks):
        span = slice(j * length, (j + 1) * length)
        value, other = pre[0][span], back[0][span]
        for l in range(1, lang_grp):
            value = jnp.where(lang == l, pre[l][span], value)
            other = jnp.where(lang == l, back[l][span], other)
        yield span, value, other


def block_marks(cots, length, units):
    found = []
    for ref in cots:
        part = ref.shape[0] - MARK
        rows = ref[part:, :units].astype(jnp.float32)
        found += [rows[j : j + 1, :] for j in range(part // length)]
    return found


def by_offset(refs, offsets, size, width, to_ref):
    place = ring_place(lax.axis_index("seq"), size)
    part = to_ref.shape[0] // len(refs)
    for at, k in enumerate(offsets):
        member = ring_member((place + k) % size, size)
        columns = pl.ds(pl.multiple_of(member * width, width), width)
        for i, ref in enumerate(refs):
            to_ref[i * part : (i + 1) * part, at * width : (at + 1) * width] = ref[:part, columns]


def first_kernel(groups, near, far, size, length, *refs):
    refs = list(refs)
    take = lambda count: [refs.pop(0) for _ in range(count)]
    rows, cots = take(groups), take(groups)
    chunks = max(1, len(near))
    downs, ups = take(chunks), take(chunks)
    x_ref, pre_ref, back_ref, c_ref = refs
    lang_grp, width, units = downs[0].shape
    if near:
        by_offset(rows, near + far, size, width, x_ref)
        by_offset(cots, near, size, width, c_ref)
    else:
        part = rows[0].shape[0]
        for i in range(groups):
            x_ref[i * part : (i + 1) * part, :] = rows[i][...]
            c_ref[i * part : (i + 1) * part, :] = cots[i][:part, :]
    marks = block_marks(cots, length, units)
    x = x_ref[:, : c_ref.shape[1]]
    for span, value, other in project(x, c_ref[...], downs, ups, marks, length, lang_grp):
        pre_ref[span, :] = value
        back_ref[span, :] = other


def gate_kernel(groups, near, far, size, length, inv_scale, *refs):
    refs = list(refs)
    take = lambda count: [refs.pop(0) for _ in range(count)]
    x_ref, pre_ref, back_ref, bias_ref = take(4)
    cots, downs, ups = take(groups), take(len(far)), take(len(far))
    g_ref = refs.pop(0)
    lang_grp, units = bias_ref.shape
    marks = block_marks(cots, length, units)
    if far:
        c_ref = refs.pop()
        width = downs[0].shape[1]
        by_offset(cots, far, size, width, c_ref)
        at = len(near) * width
        x = x_ref[:, at : at + len(far) * width]
        terms = project(x, c_ref[...], downs, ups, marks, length, lang_grp)
    else:
        terms = ((slice(j * length, (j + 1) * length), 0.0, 0.0) for j in range(len(marks)))
    for (span, value, other), lang in zip(terms, marks):
        bias = jnp.zeros((1, units), jnp.float32)
        for l in range(lang_grp):
            bias = jnp.where(lang == l, bias_ref[l : l + 1, :].astype(jnp.float32), bias)
        gate = gelu_slope(pre_ref[span, :] + value + bias) * (back_ref[span, :] + other)
        gate = gate.astype(jnp.bfloat16)
        for l in range(lang_grp):
            g_ref[span, l * units : (l + 1) * units] = jnp.where(
                lang == l, gate, jnp.zeros_like(gate)
            )
    slabs(x_ref, g_ref, refs, len(near), inv_scale)


def slabs(x_ref, g_ref, outs, skip, inv_scale):
    at = skip * 2 * outs[0].shape[0] if outs else 0
    for out_ref in outs:
        count = out_ref.shape[0]
        slab = dot(x_ref[:, at : at + count], g_ref[...], ((0,), (0,)))
        out_ref[...] = (slab * inv_scale).astype(out_ref.dtype)
        at += count


def slab_kernel(inv_scale, x_ref, g_ref, *outs):
    slabs(x_ref, g_ref, outs, 0, inv_scale)


def cycle_gather(value, size, far):
    held = {0: value}
    half = size // 2
    for way in (-1, 1):
        moving = value
        for hop in range(1, half + (1 if way == far else 0)):
            moving = lax.ppermute(moving, "seq", ring_pairs(size, -way))
            held[(way * hop) % size] = moving
    return [held[k] for k in range(size)]


def cycle_reduce(parts, size, far):
    half = size // 2
    total = parts[0].astype(jnp.float32)
    for way in (1, -1):
        hops = half if way == far else half - 1
        moving = parts[(way * hops) % size]
        for hop in range(hops - 1, -1, -1):
            moving = lax.ppermute(moving, "seq", ring_pairs(size, way))
            if hop:
                mine = parts[(way * hop) % size]
                moving = (moving.astype(jnp.float32) + mine.astype(jnp.float32)).astype(mine.dtype)
        total = total + moving.astype(jnp.float32)
    return total


def kernel(fn, **options):
    return pl.pallas_call(fn, **options)


def body(queries, keys, values, resid, w_out, block_lang, w_down, w_up, bias_down, cotangent):
    tok_dev, width_q = queries.shape
    model = resid.shape[1]
    blocks = block_lang.shape[0]
    length = tok_dev // blocks
    groups = lax.axis_size("grp")
    size = lax.axis_size("seq")
    cap = max(1, blocks // groups)
    lang_grp, _, units = w_down.shape
    bf16 = jnp.bfloat16
    late = tok_dev - WINDOW

    edge = jnp.concatenate([keys[late:], values[late:]], axis=1)
    rim = lax.ppermute(edge, "seq", [(i, i + 1) for i in range(size - 1)])

    downs = cycle_gather(w_down, size, -1)
    ups = cycle_gather(w_up, size, 1)

    cot_out = kernel(
        functools.partial(pack_kernel, groups, lang_grp),
        out_shape=[jax.ShapeDtypeStruct((cap * length + MARK, model), bf16)] * groups,
        in_specs=[SMEM, VMEM],
        out_specs=[VMEM] * groups,
    )(block_lang, cotangent.reshape(blocks, length, model))

    def exchange(messages):
        got = [messages[0]]
        for step in range(1, groups):
            pairs = [(i, peer_of(i, step, groups)) for i in range(groups)]
            got.append(lax.ppermute(messages[step], "grp", pairs))
        return got

    cots = exchange(cot_out)

    def block_spec(shape, index):
        return pl.BlockSpec(shape, lambda i: index)

    full = lambda a: block_spec(a.shape, (0,) * a.ndim)
    half_q = late // WINDOW
    rows_late = kernel(
        late_kernel,
        grid=(1,),
        out_shape=jax.ShapeDtypeStruct((late, model), bf16),
        in_specs=[
            block_spec((late, width_q), (half_q, 0)),
            full(keys),
            full(values),
            block_spec((late, model), (half_q, 0)),
            full(w_out),
        ],
        out_specs=block_spec((late, model), (0, 0)),
        scratch_shapes=[pltpu.VMEM((late, width_q), bf16)],
    )(queries, keys, values, resid, w_out)

    row_out = kernel(
        functools.partial(early_kernel, groups, lang_grp),
        grid=(1,),
        out_shape=[jax.ShapeDtypeStruct((cap * length, model), bf16)] * groups,
        in_specs=[
            SMEM,
            block_spec((WINDOW, width_q), (0, 0)),
            full(rim),
            block_spec((WINDOW, width_q), (0, 0)),
            block_spec((WINDOW, width_q), (0, 0)),
            block_spec((WINDOW, model), (0, 0)),
            full(w_out),
            full(rows_late),
        ],
        out_specs=[block_spec((cap * length, model), (0, 0))] * groups,
        scratch_shapes=[
            pltpu.VMEM((WINDOW, width_q), bf16),
            pltpu.VMEM((2 * WINDOW, width_q), bf16),
            pltpu.VMEM((2 * WINDOW, width_q), bf16),
            pltpu.VMEM((blocks, length, model), bf16),
        ],
    )(block_lang, queries, rim, keys, values, resid, w_out, rows_late)
    rows = exchange(row_out)

    share = model // size
    whole = share % LANES != 0
    cells = lang_grp * units
    half = size // 2
    near, far = [], []
    if whole:
        place = ring_place(lax.axis_index("seq"), size)
        at_offset = ring_member((place + jnp.arange(size)) % size, size)
        of_member = jnp.argsort(at_offset)
        stack = jnp.take(jnp.stack(downs), of_member, axis=0)
        downs = [stack.transpose(1, 0, 2, 3).reshape(lang_grp, model, units)]
        stack = jnp.take(jnp.stack(ups), of_member, axis=0)
        ups = [stack.transpose(1, 2, 0, 3).reshape(lang_grp, units, model)]
        downs_near, ups_near, downs_far, ups_far = downs, ups, [], []
        far_rows, near_rows = [], [model]
        near_width = model
    else:
        far = [half, half - 1, half + 1]
        near = [k for k in range(size) if k not in far]
        pick = lambda held, offsets: [held[k] for k in offsets]
        downs_near, ups_near = pick(downs, near), pick(ups, near)
        downs_far, ups_far = pick(downs, far), pick(ups, far)
        far_rows, near_rows = [share // 2] * (2 * len(far)), [share // 2] * (2 * len(near))
        near_width = share * len(near)
    tokens = groups * cap * length
    struct = jax.ShapeDtypeStruct
    x_all, pre, back = kernel(
        functools.partial(first_kernel, groups, near, far, size, length),
        out_shape=[
            struct((tokens, model), bf16),
            struct((tokens, units), jnp.float32),
            struct((tokens, units), jnp.float32),
        ],
        in_specs=[VMEM] * (2 * groups + 2 * len(downs_near)),
        out_specs=[VMEM] * 3,
        scratch_shapes=[pltpu.VMEM((tokens, near_width), bf16)],
    )(*rows, *cots, *downs_near, *ups_near)
    inv_scale = 1.0 / math.sqrt(tok_dev * size)
    gate, *far_slabs = kernel(
        functools.partial(gate_kernel, groups, near, far, size, length, inv_scale),
        out_shape=[struct((tokens, cells), bf16)] + [struct((c, cells), bf16) for c in far_rows],
        in_specs=[VMEM] * (4 + groups + 2 * len(far)),
        out_specs=[VMEM] * (1 + len(far_rows)),
        scratch_shapes=[pltpu.VMEM((tokens, share * len(far)), bf16)] if far else [],
    )(x_all, pre, back, bias_down, *cots, *downs_far, *ups_far)
    near_slabs = kernel(
        functools.partial(slab_kernel, inv_scale),
        out_shape=[struct((c, cells), bf16) for c in near_rows],
        in_specs=[VMEM] * 2,
        out_specs=[VMEM] * len(near_rows),
    )(x_all, gate)
    if whole:
        cut = jnp.take(near_slabs[0].reshape(size, 2, share // 2, cells), at_offset, axis=0)
        parts = [[cut[k, h] for k in range(size)] for h in range(2)]
    else:
        parts = []
        for h in range(2):
            found = dict(zip(near, near_slabs[h::2])) | dict(zip(far, far_slabs[h::2]))
            parts.append([found[k] for k in range(size)])
    upper = cycle_reduce(parts[0], size, 1)
    lower = cycle_reduce(parts[1], size, -1)
    return jnp.concatenate([upper, lower], axis=0).reshape(share, lang_grp, units)


def solution(mesh):
    in_specs = (
        P(("grp", "seq"), None),
        P(("grp", "seq"), None),
        P(("grp", "seq"), None),
        P(("grp", "seq"), None),
        P(),
        P(("grp", "seq")),
        P("grp", "seq", None),
        P("grp", None, "seq"),
        P("grp", None),
        P(("grp", "seq"), None),
    )
    out_specs = P("seq", "grp", None)

    return jax.shard_map(body, mesh=mesh, in_specs=in_specs, out_specs=out_specs, check_vma=False)
```

profile of v0, /device:TPU:0, one launch (start us, length us, event | category | flops | bytes accessed | tf_op | source)
XLA Modules:
  0.0 119.0 jit_solution(16196458447597044176)
XLA Ops:
  0.0 2.6 %shard_map.102 = (bf16[144,1024]{1,0:T(8,128)(2,1)}, bf16[144,1024]{1,0:T(8,128)(2,1)}, bf16[144,1024]{1,0:T(8,128)(2,1)}, bf16[144,1024]{1,0:T(8,128)(2,1)}) custom-call(s32[8]{0:T(128)} %lang_ref.3, bf16[8,64,1024]{2,1,0:T(8,128)(2,1)} %bitcast.3), custom_call_target="tpu_custom_call" | custom-call | tf_op jit(solution)/shard_map/pallas_call | solution.py:317
  2.6 0.5 collective-permute-start.4
  3.1 2.5 %collective-permute-start.5 = (bf16[144,1024]{1,0:T(8,128)(2,1)}, bf16[144,1024]{1,0:T(8,128)(2,1)S(1)}, u32[]{:S(2)}, u32[]{:S(2)}) collective-permute-start(bf16[144,1024]{1,0:T(8,128)(2,1)} %get-tuple-element.39), channel_id=1, source_target_pairs={{0,16},{8,24},{16,0},{24,8},{1,17},{9,25},{17,1},{25,9},{2,18},{10... | collective-permute-start | bytes 884744 | tf_op jit(solution)/shard_map/ppermute | solution.py:328
  5.7 1.5 %collective-permute-start.11 = (bf16[3,384,128]{2,1,0:T(8,128)(2,1)}, bf16[3,384,128]{2,1,0:T(8,128)(2,1)S(1)}, u32[]{:S(2)}, u32[]{:S(2)}) collective-permute-start(bf16[3,384,128]{2,1,0:T(8,128)(2,1)} %refs_13_.1), channel_id=1, source_target_pairs={{0,1},{2,0},{4,2},{6,4},{7,6},{5,7},{3,5},{1,3},{8,9},{10,8},{12,1... | collective-permute-start | bytes 884744 | tf_op jit(solution)/shard_map/ppermute | solution.py:275
  7.1 0.5 collective-permute-start.13
  7.7 1.6 %collective-permute-start.9 = (bf16[3,128,384]{2,1,0:T(8,128)(2,1)}, bf16[3,128,384]{2,1,0:T(8,128)(2,1)S(1)}, u32[]{:S(2)}, u32[]{:S(2)}) collective-permute-start(bf16[3,128,384]{2,1,0:T(8,128)(2,1)} %refs_8_.1), channel_id=1, source_target_pairs={{0,2},{2,4},{4,6},{6,7},{7,5},{5,3},{3,1},{1,0},{8,10},{10,12},{12... | collective-permute-start | bytes 884744 | tf_op jit(solution)/shard_map/ppermute | solution.py:275
  9.3 0.5 collective-permute-start.7
  9.8 0.1 pad_maximum_fusion.1
  9.8 3.7 %collective-permute-done.5.refs_6_ = bf16[144,1024]{1,0:T(8,128)(2,1)S(1)} collective-permute-done((bf16[144,1024]{1,0:T(8,128)(2,1)}, bf16[144,1024]{1,0:T(8,128)(2,1)S(1)}, u32[]{:S(2)}, u32[]{:S(2)}) %collective-permute-start.5) | collective-permute-done | bytes 294944 | tf_op jit(solution)/shard_map/ppermute | solution.py:328
  13.5 3.6 %collective-permute-start = (bf16[256,1024]{1,0:T(8,128)(2,1)S(1)}, bf16[256,1024]{1,0:T(8,128)(2,1)S(1)}, u32[]{:S(2)}, u32[]{:S(2)}) collective-permute-start(bf16[256,1024]{1,0:T(8,128)(2,1)S(1)} %pad_maximum_fusion.1), channel_id=1, source_target_pairs={{0,1},{1,2},{2,3},{3,4},{4,5},{5,6},{6,7},{8,9},{9,10},{10,11},{11... | collective-permute-start | bytes 1572872 | tf_op jit(solution)/shard_map/ppermute | solution.py:312
  17.2 5.3 %collective-permute-done.9.refs_12_ = bf16[3,128,384]{2,1,0:T(8,128)(2,1)S(1)} collective-permute-done((bf16[3,128,384]{2,1,0:T(8,128)(2,1)}, bf16[3,128,384]{2,1,0:T(8,128)(2,1)S(1)}, u32[]{:S(2)}, u32[]{:S(2)}) %collective-permute-start.9) | collective-permute-done | bytes 294944 | tf_op jit(solution)/shard_map/ppermute | solution.py:275
  22.5 0.5 collective-permute-start.10
  23.1 1.5 %collective-permute-start.12 = (bf16[3,384,128]{2,1,0:T(8,128)(2,1)S(1)}, bf16[3,384,128]{2,1,0:T(8,128)(2,1)}, u32[]{:S(2)}, u32[]{:S(2)}) collective-permute-start(bf16[3,384,128]{2,1,0:T(8,128)(2,1)S(1)} %collective-permute-done.11.refs_14_), channel_id=1, source_target_pairs={{0,1},{2,0},{4,2},{6,4},{7,6},{5,7},{3,5},{1,3},{8,9},{10,8},{12,1... | collective-permute-start | bytes 884744 | tf_op jit(solution)/shard_map/ppermute | solution.py:275
  24.6 0.6 collective-permute-start.14
  25.2 7.1 %collective-permute-done.rim_ref = bf16[256,1024]{1,0:T(8,128)(2,1)S(1)} collective-permute-done((bf16[256,1024]{1,0:T(8,128)(2,1)S(1)}, bf16[256,1024]{1,0:T(8,128)(2,1)S(1)}, u32[]{:S(2)}, u32[]{:S(2)}) %collective-permute-start) | collective-permute-done | bytes 524320 | tf_op jit(solution)/shard_map/ppermute | solution.py:312
  32.3 2.5 %collective-permute-start.8 = (bf16[3,128,384]{2,1,0:T(8,128)(2,1)S(1)}, bf16[3,128,384]{2,1,0:T(8,128)(2,1)}, u32[]{:S(2)}, u32[]{:S(2)}) collective-permute-start(bf16[3,128,384]{2,1,0:T(8,128)(2,1)S(1)} %collective-permute-done.7.refs_9_), channel_id=1, source_target_pairs={{0,1},{2,0},{4,2},{6,4},{7,6},{5,7},{3,5},{1,3},{8,9},{10,8},{12,1... | collective-permute-start | bytes 884744 | tf_op jit(solution)/shard_map/ppermute | solution.py:275
  34.8 1.1 collective-permute-start.15
  35.9 2.8 %collective-permute-done.12.refs_15_ = bf16[3,384,128]{2,1,0:T(8,128)(2,1)} collective-permute-done((bf16[3,384,128]{2,1,0:T(8,128)(2,1)S(1)}, bf16[3,384,128]{2,1,0:T(8,128)(2,1)}, u32[]{:S(2)}, u32[]{:S(2)}) %collective-permute-start.12) | collective-permute-done | bytes 294944 | tf_op jit(solution)/shard_map/ppermute | solution.py:275
  38.6 2.6 %collective-permute-start.18 = (bf16[3,384,128]{2,1,0:T(8,128)(2,1)}, bf16[3,384,128]{2,1,0:T(8,128)(2,1)}, u32[]{:S(2)}, u32[]{:S(2)}) collective-permute-start(bf16[3,384,128]{2,1,0:T(8,128)(2,1)} %collective-permute-done.12.refs_15_), channel_id=1, source_target_pairs={{0,1},{2,0},{4,2},{6,4},{7,6},{5,7},{3,5},{1,3},{8,9},{10,8},{12,1... | collective-permute-start | bytes 884744 | tf_op jit(solution)/shard_map/ppermute | solution.py:275
  41.2 5.0 %shard_map.100.late_ref = bf16[256,1024]{1,0:T(8,128)(2,1)} custom-call(bf16[512,512]{1,0:T(8,128)(2,1)} %q_ref.3, bf16[512,512]{1,0:T(8,128)(2,1)} %k_ref.3, bf16[512,512]{1,0:T(8,128)(2,1)} %v_ref.3, bf16[512,1024]{1,0:T(8,128)(2,1)} %r_ref.3, bf16[512,1024]{1,0:T(8,128)(2,1)} %wo_ref.3), custom_call_target="tpu_custom_call" | custom-call | tf_op jit(solution)/shard_map/pallas_call | solution.py:338
  46.3 5.4 %shard_map.101 = (bf16[128,1024]{1,0:T(8,128)(2,1)}, bf16[128,1024]{1,0:T(8,128)(2,1)}, bf16[128,1024]{1,0:T(8,128)(2,1)}, bf16[128,1024]{1,0:T(8,128)(2,1)}) custom-call(s32[8]{0:T(128)} %lang_ref.3, bf16[512,512]{1,0:T(8,128)(2,1)} %q_ref.3, bf16[256,1024]{1,0:T(8,128)(2,1)} %copy-done.3, bf16[512,512]{1,0:T(8,128)(2,1)} %k_ref.3, bf16[512,512]{1,0:T(8,128)(2,1)} %v_ref.3, ...), custom_call_target="tpu_custom_call" | custom-call | tf_op jit(solution)/shard_map/pallas_call | solution.py:353
  51.7 0.1 collective-permute-start.1
  51.8 0.6 collective-permute-start.2
  52.4 1.6 %collective-permute-start.17 = (bf16[3,128,384]{2,1,0:T(8,128)(2,1)}, bf16[3,128,384]{2,1,0:T(8,128)(2,1)S(1)}, u32[]{:S(2)}, u32[]{:S(2)}) collective-permute-start(bf16[3,128,384]{2,1,0:T(8,128)(2,1)} %collective-permute-done.8.refs_10_), channel_id=1, source_target_pairs={{0,1},{2,0},{4,2},{6,4},{7,6},{5,7},{3,5},{1,3},{8,9},{10,8},{12,1... | collective-permute-start | bytes 884744 | tf_op jit(solution)/shard_map/ppermute | solution.py:275
  54.0 0.4 collective-permute-start.20
  54.5 1.8 %collective-permute-start.16 = (bf16[3,128,384]{2,1,0:T(8,128)(2,1)S(1)}, bf16[3,128,384]{2,1,0:T(8,128)(2,1)S(1)}, u32[]{:S(2)}, u32[]{:S(2)}) collective-permute-start(bf16[3,128,384]{2,1,0:T(8,128)(2,1)S(1)} %collective-permute-done.15.refs_10_), channel_id=1, source_target_pairs={{0,2},{2,4},{4,6},{6,7},{7,5},{5,3},{3,1},{1,0},{8,10},{10,12},{12... | collective-permute-start | bytes 884744 | tf_op jit(solution)/shard_map/ppermute | solution.py:275
  56.3 0.2 collective-permute-start.19
  56.5 4.3 %collective-permute-done.2.refs_2_ = bf16[128,1024]{1,0:T(8,128)(2,1)S(1)} collective-permute-done((bf16[128,1024]{1,0:T(8,128)(2,1)}, bf16[128,1024]{1,0:T(8,128)(2,1)S(1)}, u32[]{:S(2)}, u32[]{:S(2)}) %collective-permute-start.2) | collective-permute-done | bytes 262176 | tf_op jit(solution)/shard_map/ppermute | solution.py:328
  60.8 8.6 %collective-permute-done.3.refs_3_ = bf16[128,1024]{1,0:T(8,128)(2,1)S(1)} collective-permute-done((bf16[128,1024]{1,0:T(8,128)(2,1)}, bf16[128,1024]{1,0:T(8,128)(2,1)S(1)}, u32[]{:S(2)}, u32[]{:S(2)}) %collective-permute-start.3) | collective-permute-done | bytes 262176 | tf_op jit(solution)/shard_map/ppermute | solution.py:328
  69.3 0.7 copy-done.17
  70.0 5.9 %shard_map.103 = (bf16[512,1024]{1,0:T(8,128)(2,1)}, f32[512,384]{1,0:T(8,128)}, f32[512,384]{1,0:T(8,128)}) custom-call(bf16[128,1024]{1,0:T(8,128)(2,1)} %get-tuple-element.33.refs_0_, bf16[128,1024]{1,0:T(8,128)(2,1)} %copy-done.15, bf16[128,1024]{1,0:T(8,128)(2,1)} %copy-done.16, bf16[128,1024]{1,0:T(8,128)(2,1)} %copy-done.17, ...), custom_call_target="tpu_custom_call" | custom-call | tf_op jit(solution)/shard_map/pallas_call | solution.py:403
  76.1 0.6 copy-done.11
  76.7 0.2 copy-done.12
  76.9 0.1 copy-done.13
  77.0 0.1 copy-done.14
  77.0 6.6 %shard_map.104 = (bf16[512,1152]{1,0:T(8,128)(2,1)}, bf16[64,1152]{1,0:T(8,128)(2,1)}, bf16[64,1152]{1,0:T(8,128)(2,1)}, bf16[64,1152]{1,0:T(8,128)(2,1)}, bf16[...) custom-call(bf16[512,1024]{1,0:T(8,128)(2,1)} %get-tuple-element.41.refs_0_.x_ref, ...), custom_call_target="tpu_custom_call" | custom-call | tf_op jit(solution)/shard_map/pallas_call | solution.py:415
  83.7 0.1 collective-permute-start.21
  83.7 4.6 %shard_map.105 = (bf16[64,1152]{1,0:T(8,128)(2,1)}, bf16[64,1152]{1,0:T(8,128)(2,1)}, bf16[64,1152]{1,0:T(8,128)(2,1)}, bf16[64,1152]{1,0:T(8,128)(2,1)}, bf16[6...) custom-call(bf16[512,1024]{1,0:T(8,128)(2,1)} %get-tuple-element.41., ...), custom_call_target="tpu_custom_call" | custom-call | tf_op jit(solution)/shard_map/pallas_call | solution.py:422
  88.3 1.9 %collective-permute-start.25 = (bf16[64,1152]{1,0:T(8,128)(2,1)S(1)}, bf16[64,1152]{1,0:T(8,128)(2,1)S(1)}, u32[]{:S(2)}, u32[]{:S(2)}) collective-permute-start(bf16[64,1152]{1,0:T(8,128)(2,1)S(1)} %copy-done.30), channel_id=1, source_target_pairs={{0,1},{2,0},{4,2},{6,4},{7,6},{5,7},{3,5},{1,3},{8,9},{10,8},{12,1... | collective-permute-start | bytes 442376 | tf_op jit(solution)/shard_map/ppermute | solution.py:287
  90.3 0.8 collective-permute-start.28
  91.0 1.3 %collective-permute-start.31 = (bf16[64,1152]{1,0:T(8,128)(2,1)S(1)}, bf16[64,1152]{1,0:T(8,128)(2,1)S(1)}, u32[]{:S(2)}, u32[]{:S(2)}) collective-permute-start(bf16[64,1152]{1,0:T(8,128)(2,1)S(1)} %copy-done.28), channel_id=1, source_target_pairs={{0,1},{2,0},{4,2},{6,4},{7,6},{5,7},{3,5},{1,3},{8,9},{10,8},{12,1... | collective-permute-start | bytes 442376 | tf_op jit(solution)/shard_map/ppermute | solution.py:287
  92.4 1.3 %collective-permute-start.22 = (bf16[64,1152]{1,0:T(8,128)(2,1)S(1)}, bf16[64,1152]{1,0:T(8,128)(2,1)S(1)}, u32[]{:S(2)}, u32[]{:S(2)}) collective-permute-start(bf16[64,1152]{1,0:T(8,128)(2,1)S(1)} %add_convert_fusion.9), channel_id=1, source_target_pairs={{0,2},{2,4},{4,6},{6,7},{7,5},{5,3},{3,1},{1,0},{8,10},{10,12},{12... | collective-permute-start | bytes 442376 | tf_op jit(solution)/shard_map/ppermute | solution.py:287
  93.6 1.8 %collective-permute-done.25 = bf16[64,1152]{1,0:T(8,128)(2,1)S(1)} collective-permute-done((bf16[64,1152]{1,0:T(8,128)(2,1)S(1)}, bf16[64,1152]{1,0:T(8,128)(2,1)S(1)}, u32[]{:S(2)}, u32[]{:S(2)}) %collective-permute-start.25) | collective-permute-done | bytes 147488 | tf_op jit(solution)/shard_map/ppermute | solution.py:287
  95.4 0.9 add_convert_fusion.6
  96.4 1.6 %collective-permute-start.26 = (bf16[64,1152]{1,0:T(8,128)(2,1)S(1)}, bf16[64,1152]{1,0:T(8,128)(2,1)S(1)}, u32[]{:S(2)}, u32[]{:S(2)}) collective-permute-start(bf16[64,1152]{1,0:T(8,128)(2,1)S(1)} %add_convert_fusion.6), channel_id=1, source_target_pairs={{0,1},{2,0},{4,2},{6,4},{7,6},{5,7},{3,5},{1,3},{8,9},{10,8},{12,1... | collective-permute-start | bytes 442376 | tf_op jit(solution)/shard_map/ppermute | solution.py:287
  98.0 0.9 add_convert_fusion.4
  99.0 1.2 %collective-permute-start.29 = (bf16[64,1152]{1,0:T(8,128)(2,1)S(1)}, bf16[64,1152]{1,0:T(8,128)(2,1)S(1)}, u32[]{:S(2)}, u32[]{:S(2)}) collective-permute-start(bf16[64,1152]{1,0:T(8,128)(2,1)S(1)} %add_convert_fusion.4), channel_id=1, source_target_pairs={{0,2},{2,4},{4,6},{6,7},{7,5},{5,3},{3,1},{1,0},{8,10},{10,12},{12... | collective-permute-start | bytes 442376 | tf_op jit(solution)/shard_map/ppermute | solution.py:287
  100.2 0.9 collective-permute-start.32
  101.2 1.2 %collective-permute-start.23 = (bf16[64,1152]{1,0:T(8,128)(2,1)S(1)}, bf16[64,1152]{1,0:T(8,128)(2,1)S(1)}, u32[]{:S(2)}, u32[]{:S(2)}) collective-permute-start(bf16[64,1152]{1,0:T(8,128)(2,1)S(1)} %add_convert_fusion.8), channel_id=1, source_target_pairs={{0,2},{2,4},{4,6},{6,7},{7,5},{5,3},{3,1},{1,0},{8,10},{10,12},{12... | collective-permute-start | bytes 442376 | tf_op jit(solution)/shard_map/ppermute | solution.py:287
  102.5 1.3 %collective-permute-done.26 = bf16[64,1152]{1,0:T(8,128)(2,1)S(1)} collective-permute-done((bf16[64,1152]{1,0:T(8,128)(2,1)S(1)}, bf16[64,1152]{1,0:T(8,128)(2,1)S(1)}, u32[]{:S(2)}, u32[]{:S(2)}) %collective-permute-start.26) | collective-permute-done | bytes 147488 | tf_op jit(solution)/shard_map/ppermute | solution.py:287
  103.8 1.0 collective-permute-start.27
  104.8 0.0 collective-permute-done.29
  104.9 2.1 %collective-permute-start.30 = (bf16[64,1152]{1,0:T(8,128)(2,1)S(1)}, bf16[64,1152]{1,0:T(8,128)(2,1)S(1)}, u32[]{:S(2)}, u32[]{:S(2)}) collective-permute-start(bf16[64,1152]{1,0:T(8,128)(2,1)S(1)} %add_convert_fusion.3), channel_id=1, source_target_pairs={{0,2},{2,4},{4,6},{6,7},{7,5},{5,3},{3,1},{1,0},{8,10},{10,12},{12... | collective-permute-start | bytes 442376 | tf_op jit(solution)/shard_map/ppermute | solution.py:287
  107.1 0.3 collective-permute-start.33
  107.3 0.5 collective-permute-done.23
  107.9 1.7 %collective-permute-start.24 = (bf16[64,1152]{1,0:T(8,128)(2,1)S(1)}, bf16[64,1152]{1,0:T(8,128)(2,1)S(1)}, u32[]{:S(2)}, u32[]{:S(2)}) collective-permute-start(bf16[64,1152]{1,0:T(8,128)(2,1)S(1)} %add_convert_fusion.7), channel_id=1, source_target_pairs={{0,2},{2,4},{4,6},{6,7},{7,5},{5,3},{3,1},{1,0},{8,10},{10,12},{12... | collective-permute-start | bytes 442376 | tf_op jit(solution)/shard_map/ppermute | solution.py:287
  109.6 2.7 %collective-permute-done.33 = bf16[64,1152]{1,0:T(8,128)(2,1)S(1)} collective-permute-done((bf16[64,1152]{1,0:T(8,128)(2,1)S(1)}, bf16[64,1152]{1,0:T(8,128)(2,1)S(1)}, u32[]{:S(2)}, u32[]{:S(2)}) %collective-permute-start.33) | collective-permute-done | bytes 147488 | tf_op jit(solution)/shard_map/ppermute | solution.py:287
  112.3 0.5 collective-permute-start.34
  112.8 0.3 collective-permute-done.24
  113.1 0.1 convert_add_fusion.1
  113.2 4.5 %collective-permute-done.34 = bf16[64,1152]{1,0:T(8,128)(2,1)S(1)} collective-permute-done((bf16[64,1152]{1,0:T(8,128)(2,1)S(1)}, bf16[64,1152]{1,0:T(8,128)(2,1)S(1)}, u32[]{:S(2)}, u32[]{:S(2)}) %collective-permute-start.34) | collective-permute-done | bytes 147488 | tf_op jit(solution)/shard_map/ppermute | solution.py:287
  117.6 0.1 convert_add_fusion
  117.7 0.2 copy.12
  118.0 1.1 copy.13
  (94 shorter events, 0.5 us)
Async XLA Ops:
  0.0 9.3 %copy-start.4 = (bf16[3,128,384]{2,1,0:T(8,128)(2,1)S(1)}, bf16[3,128,384]{2,1,0:T(8,128)(2,1)}, u32[]{:S(2)}) copy-start(bf16[3,128,384]{2,1,0:T(8,128)(2,1)} %refs_8_.1) | copy-start | bytes 884740
  0.0 9.8 %slice-start.1 = ((bf16[512,512]{1,0:T(8,128)(2,1)}), bf16[256,512]{1,0:T(8,128)(2,1)S(1)}, s32[]{:S(2)}) async-start(bf16[512,512]{1,0:T(8,128)(2,1)} %k_ref.3), calls=%async_computation.1 | async-start | bytes 524288 | tf_op jit(solution)/shard_map/slice | solution.py:311
  0.0 9.8 %slice-start = ((bf16[512,512]{1,0:T(8,128)(2,1)}), bf16[256,512]{1,0:T(8,128)(2,1)S(1)}, s32[]{:S(2)}) async-start(bf16[512,512]{1,0:T(8,128)(2,1)} %v_ref.3), calls=%async_computation | async-start | bytes 524288 | tf_op jit(solution)/shard_map/slice | solution.py:311
  2.6 6.6 %collective-permute-start.4 = (bf16[144,1024]{1,0:T(8,128)(2,1)}, bf16[144,1024]{1,0:T(8,128)(2,1)S(1)}, u32[]{:S(2)}, u32[]{:S(2)}) collective-permute-start(bf16[144,1024]{1,0:T(8,128)(2,1)} %get-tuple-element.38), channel_id=1, source_target_pairs={{0,8},{8,0},{16,24},{24,16},{1,9},{9,1},{17,25},{25,17},{2,10},{10... | collective-permute-start | bytes 884744 | tf_op jit(solution)/shard_map/ppermute | solution.py:328
  3.1 10.4 %collective-permute-start.5 = (bf16[144,1024]{1,0:T(8,128)(2,1)}, bf16[144,1024]{1,0:T(8,128)(2,1)S(1)}, u32[]{:S(2)}, u32[]{:S(2)}) collective-permute-start(bf16[144,1024]{1,0:T(8,128)(2,1)} %get-tuple-element.39), channel_id=1, source_target_pairs={{0,16},{8,24},{16,0},{24,8},{1,17},{9,25},{17,1},{25,9},{2,18},{10... | collective-permute-start | bytes 884744 | tf_op jit(solution)/shard_map/ppermute | solution.py:328
  5.7 17.4 %collective-permute-start.11 = (bf16[3,384,128]{2,1,0:T(8,128)(2,1)}, bf16[3,384,128]{2,1,0:T(8,128)(2,1)S(1)}, u32[]{:S(2)}, u32[]{:S(2)}) collective-permute-start(bf16[3,384,128]{2,1,0:T(8,128)(2,1)} %refs_13_.1), channel_id=1, source_target_pairs={{0,1},{2,0},{4,2},{6,4},{7,6},{5,7},{3,5},{1,3},{8,9},{10,8},{12,1... | collective-permute-start | bytes 884744 | tf_op jit(solution)/shard_map/ppermute | solution.py:275
  7.1 17.4 %collective-permute-start.13 = (bf16[3,384,128]{2,1,0:T(8,128)(2,1)}, bf16[3,384,128]{2,1,0:T(8,128)(2,1)S(1)}, u32[]{:S(2)}, u32[]{:S(2)}) collective-permute-start(bf16[3,384,128]{2,1,0:T(8,128)(2,1)} %refs_13_.1), channel_id=1, source_target_pairs={{0,2},{2,4},{4,6},{6,7},{7,5},{5,3},{3,1},{1,0},{8,10},{10,12},{12... | collective-permute-start | bytes 884744 | tf_op jit(solution)/shard_map/ppermute | solution.py:275
  7.7 14.9 %collective-permute-start.9 = (bf16[3,128,384]{2,1,0:T(8,128)(2,1)}, bf16[3,128,384]{2,1,0:T(8,128)(2,1)S(1)}, u32[]{:S(2)}, u32[]{:S(2)}) collective-permute-start(bf16[3,128,384]{2,1,0:T(8,128)(2,1)} %refs_8_.1), channel_id=1, source_target_pairs={{0,2},{2,4},{4,6},{6,7},{7,5},{5,3},{3,1},{1,0},{8,10},{10,12},{12... | collective-permute-start | bytes 884744 | tf_op jit(solution)/shard_map/ppermute | solution.py:275
  9.3 37.0 %copy-start = (bf16[144,1024]{1,0:T(8,128)(2,1)}, bf16[144,1024]{1,0:T(8,128)(2,1)S(1)}, u32[]{:S(2)}) copy-start(bf16[144,1024]{1,0:T(8,128)(2,1)S(1)} %collective-permute-done.4.refs_5_) | copy-start | bytes 884740
  9.3 15.3 %collective-permute-start.7 = (bf16[3,128,384]{2,1,0:T(8,128)(2,1)S(1)}, bf16[3,128,384]{2,1,0:T(8,128)(2,1)S(1)}, u32[]{:S(2)}, u32[]{:S(2)}) collective-permute-start(bf16[3,128,384]{2,1,0:T(8,128)(2,1)S(1)} %copy-done.4), channel_id=1, source_target_pairs={{0,1},{2,0},{4,2},{6,4},{7,6},{5,7},{3,5},{1,3},{8,9},{10,8},{12,1... | collective-permute-start | bytes 884744 | tf_op jit(solution)/shard_map/ppermute | solution.py:275
  13.5 32.7 %copy-start.1 = (bf16[144,1024]{1,0:T(8,128)(2,1)}, bf16[144,1024]{1,0:T(8,128)(2,1)S(1)}, u32[]{:S(2)}) copy-start(bf16[144,1024]{1,0:T(8,128)(2,1)S(1)} %collective-permute-done.5.refs_6_) | copy-start | bytes 884740
  13.5 18.8 %collective-permute-start = (bf16[256,1024]{1,0:T(8,128)(2,1)S(1)}, bf16[256,1024]{1,0:T(8,128)(2,1)S(1)}, u32[]{:S(2)}, u32[]{:S(2)}) collective-permute-start(bf16[256,1024]{1,0:T(8,128)(2,1)S(1)} %pad_maximum_fusion.1), channel_id=1, source_target_pairs={{0,1},{1,2},{2,3},{3,4},{4,5},{5,6},{6,7},{8,9},{9,10},{10,11},{11... | collective-permute-start | bytes 1572872 | tf_op jit(solution)/shard_map/ppermute | solution.py:312
  22.5 23.7 %copy-start.7 = (bf16[3,128,384]{2,1,0:T(8,128)(2,1)}, bf16[3,128,384]{2,1,0:T(8,128)(2,1)S(1)}, u32[]{:S(2)}) copy-start(bf16[3,128,384]{2,1,0:T(8,128)(2,1)S(1)} %collective-permute-done.9.refs_12_) | copy-start | bytes 884740
  22.5 12.3 %collective-permute-start.10 = (bf16[3,128,384]{2,1,0:T(8,128)(2,1)S(1)}, bf16[3,128,384]{2,1,0:T(8,128)(2,1)S(1)}, u32[]{:S(2)}, u32[]{:S(2)}) collective-permute-start(bf16[3,128,384]{2,1,0:T(8,128)(2,1)S(1)} %collective-permute-done.9.refs_12_), channel_id=1, source_target_pairs={{0,2},{2,4},{4,6},{6,7},{7,5},{5,3},{3,1},{1,0},{8,10},{10,12},{12... | collective-permute-start | bytes 884744 | tf_op jit(solution)/shard_map/ppermute | solution.py:275
  23.1 23.2 %copy-start.5 = (bf16[3,384,128]{2,1,0:T(8,128)(2,1)}, bf16[3,384,128]{2,1,0:T(8,128)(2,1)S(1)}, u32[]{:S(2)}) copy-start(bf16[3,384,128]{2,1,0:T(8,128)(2,1)S(1)} %collective-permute-done.11.refs_14_) | copy-start | bytes 884740
  23.1 15.6 %collective-permute-start.12 = (bf16[3,384,128]{2,1,0:T(8,128)(2,1)S(1)}, bf16[3,384,128]{2,1,0:T(8,128)(2,1)}, u32[]{:S(2)}, u32[]{:S(2)}) collective-permute-start(bf16[3,384,128]{2,1,0:T(8,128)(2,1)S(1)} %collective-permute-done.11.refs_14_), channel_id=1, source_target_pairs={{0,1},{2,0},{4,2},{6,4},{7,6},{5,7},{3,5},{1,3},{8,9},{10,8},{12,1... | collective-permute-start | bytes 884744 | tf_op jit(solution)/shard_map/ppermute | solution.py:275
  24.6 21.7 %copy-start.6 = (bf16[3,384,128]{2,1,0:T(8,128)(2,1)}, bf16[3,384,128]{2,1,0:T(8,128)(2,1)S(1)}, u32[]{:S(2)}) copy-start(bf16[3,384,128]{2,1,0:T(8,128)(2,1)S(1)} %collective-permute-done.13.refs_17_) | copy-start | bytes 884740
  24.6 27.2 %collective-permute-start.6 = (bf16[144,1024]{1,0:T(8,128)(2,1)}, bf16[144,1024]{1,0:T(8,128)(2,1)S(1)}, u32[]{:S(2)}, u32[]{:S(2)}) collective-permute-start(bf16[144,1024]{1,0:T(8,128)(2,1)} %get-tuple-element.40), channel_id=1, source_target_pairs={{0,24},{8,16},{16,8},{24,0},{1,25},{9,17},{17,9},{25,1},{2,26},{10... | collective-permute-start | bytes 884744 | tf_op jit(solution)/shard_map/ppermute | solution.py:328
  24.6 21.7 %copy-start.8 = (bf16[3,128,384]{2,1,0:T(8,128)(2,1)}, bf16[3,128,384]{2,1,0:T(8,128)(2,1)S(1)}, u32[]{:S(2)}) copy-start(bf16[3,128,384]{2,1,0:T(8,128)(2,1)S(1)} %collective-permute-done.7.refs_9_) | copy-start | bytes 884740
  24.6 27.2 %collective-permute-start.14 = (bf16[3,384,128]{2,1,0:T(8,128)(2,1)S(1)}, bf16[3,384,128]{2,1,0:T(8,128)(2,1)}, u32[]{:S(2)}, u32[]{:S(2)}) collective-permute-start(bf16[3,384,128]{2,1,0:T(8,128)(2,1)S(1)} %collective-permute-done.13.refs_17_), channel_id=1, source_target_pairs={{0,2},{2,4},{4,6},{6,7},{7,5},{5,3},{3,1},{1,0},{8,10},{10,12},{12... | collective-permute-start | bytes 884744 | tf_op jit(solution)/shard_map/ppermute | solution.py:275
  32.3 14.0 %copy-start.3 = (bf16[256,1024]{1,0:T(8,128)(2,1)}, bf16[256,1024]{1,0:T(8,128)(2,1)S(1)}, u32[]{:S(2)}) copy-start(bf16[256,1024]{1,0:T(8,128)(2,1)S(1)} %collective-permute-done.rim_ref) | copy-start | bytes 1572868
  32.3 20.1 %collective-permute-start.8 = (bf16[3,128,384]{2,1,0:T(8,128)(2,1)S(1)}, bf16[3,128,384]{2,1,0:T(8,128)(2,1)}, u32[]{:S(2)}, u32[]{:S(2)}) collective-permute-start(bf16[3,128,384]{2,1,0:T(8,128)(2,1)S(1)} %collective-permute-done.7.refs_9_), channel_id=1, source_target_pairs={{0,1},{2,0},{4,2},{6,4},{7,6},{5,7},{3,5},{1,3},{8,9},{10,8},{12,1... | collective-permute-start | bytes 884744 | tf_op jit(solution)/shard_map/ppermute | solution.py:275
  34.8 11.5 %copy-start.9 = (bf16[3,128,384]{2,1,0:T(8,128)(2,1)}, bf16[3,128,384]{2,1,0:T(8,128)(2,1)S(1)}, u32[]{:S(2)}) copy-start(bf16[3,128,384]{2,1,0:T(8,128)(2,1)S(1)} %collective-permute-done.10.refs_11_) | copy-start | bytes 884740
  34.8 19.6 %collective-permute-start.15 = (bf16[3,128,384]{2,1,0:T(8,128)(2,1)S(1)}, bf16[3,128,384]{2,1,0:T(8,128)(2,1)S(1)}, u32[]{:S(2)}, u32[]{:S(2)}) collective-permute-start(bf16[3,128,384]{2,1,0:T(8,128)(2,1)S(1)} %collective-permute-done.10.refs_11_), channel_id=1, source_target_pairs={{0,2},{2,4},{4,6},{6,7},{7,5},{5,3},{3,1},{1,0},{8,10},{10,12},{12... | collective-permute-start | bytes 884744 | tf_op jit(solution)/shard_map/ppermute | solution.py:275
  38.6 17.6 %collective-permute-start.18 = (bf16[3,384,128]{2,1,0:T(8,128)(2,1)}, bf16[3,384,128]{2,1,0:T(8,128)(2,1)}, u32[]{:S(2)}, u32[]{:S(2)}) collective-permute-start(bf16[3,384,128]{2,1,0:T(8,128)(2,1)} %collective-permute-done.12.refs_15_), channel_id=1, source_target_pairs={{0,1},{2,0},{4,2},{6,4},{7,6},{5,7},{3,5},{1,3},{8,9},{10,8},{12,1... | collective-permute-start | bytes 884744 | tf_op jit(solution)/shard_map/ppermute | solution.py:275
  51.7 17.6 %copy-start.2 = (bf16[144,1024]{1,0:T(8,128)(2,1)}, bf16[144,1024]{1,0:T(8,128)(2,1)S(1)}, u32[]{:S(2)}) copy-start(bf16[144,1024]{1,0:T(8,128)(2,1)S(1)} %collective-permute-done.6.refs_7_) | copy-start | bytes 884740
  51.7 2.3 %collective-permute-start.1 = (bf16[128,1024]{1,0:T(8,128)(2,1)}, bf16[128,1024]{1,0:T(8,128)(2,1)S(1)}, u32[]{:S(2)}, u32[]{:S(2)}) collective-permute-start(bf16[128,1024]{1,0:T(8,128)(2,1)} %get-tuple-element.34), channel_id=1, source_target_pairs={{0,8},{8,0},{16,24},{24,16},{1,9},{9,1},{17,25},{25,17},{2,10},{10... | collective-permute-start | bytes 786440 | tf_op jit(solution)/shard_map/ppermute | solution.py:328
  51.8 8.9 %collective-permute-start.2 = (bf16[128,1024]{1,0:T(8,128)(2,1)}, bf16[128,1024]{1,0:T(8,128)(2,1)S(1)}, u32[]{:S(2)}, u32[]{:S(2)}) collective-permute-start(bf16[128,1024]{1,0:T(8,128)(2,1)} %get-tuple-element.35), channel_id=1, source_target_pairs={{0,16},{8,24},{16,0},{24,8},{1,17},{9,25},{17,1},{25,9},{2,18},{10... | collective-permute-start | bytes 786440 | tf_op jit(solution)/shard_map/ppermute | solution.py:328
  52.4 23.6 %collective-permute-start.17 = (bf16[3,128,384]{2,1,0:T(8,128)(2,1)}, bf16[3,128,384]{2,1,0:T(8,128)(2,1)S(1)}, u32[]{:S(2)}, u32[]{:S(2)}) collective-permute-start(bf16[3,128,384]{2,1,0:T(8,128)(2,1)} %collective-permute-done.8.refs_10_), channel_id=1, source_target_pairs={{0,1},{2,0},{4,2},{6,4},{7,6},{5,7},{3,5},{1,3},{8,9},{10,8},{12,1... | collective-permute-start | bytes 884744 | tf_op jit(solution)/shard_map/ppermute | solution.py:275
  54.0 15.3 %copy-start.15 = (bf16[128,1024]{1,0:T(8,128)(2,1)}, bf16[128,1024]{1,0:T(8,128)(2,1)S(1)}, u32[]{:S(2)}) copy-start(bf16[128,1024]{1,0:T(8,128)(2,1)S(1)} %collective-permute-done.1.refs_1_) | copy-start | bytes 786436
  54.0 22.0 %collective-permute-start.20 = (bf16[3,384,128]{2,1,0:T(8,128)(2,1)}, bf16[3,384,128]{2,1,0:T(8,128)(2,1)S(1)}, u32[]{:S(2)}, u32[]{:S(2)}) collective-permute-start(bf16[3,384,128]{2,1,0:T(8,128)(2,1)} %collective-permute-done.14.refs_16_), channel_id=1, source_target_pairs={{0,2},{2,4},{4,6},{6,7},{7,5},{5,3},{3,1},{1,0},{8,10},{10,12},{12... | collective-permute-start | bytes 884744 | tf_op jit(solution)/shard_map/ppermute | solution.py:275
  54.4 21.5 %copy-start.10 = (bf16[3,128,384]{2,1,0:T(8,128)(2,1)}, bf16[3,128,384]{2,1,0:T(8,128)(2,1)S(1)}, u32[]{:S(2)}) copy-start(bf16[3,128,384]{2,1,0:T(8,128)(2,1)S(1)} %collective-permute-done.15.refs_10_) | copy-start | bytes 884740
  54.5 21.6 %collective-permute-start.16 = (bf16[3,128,384]{2,1,0:T(8,128)(2,1)S(1)}, bf16[3,128,384]{2,1,0:T(8,128)(2,1)S(1)}, u32[]{:S(2)}, u32[]{:S(2)}) collective-permute-start(bf16[3,128,384]{2,1,0:T(8,128)(2,1)S(1)} %collective-permute-done.15.refs_10_), channel_id=1, source_target_pairs={{0,2},{2,4},{4,6},{6,7},{7,5},{5,3},{3,1},{1,0},{8,10},{10,12},{12... | collective-permute-start | bytes 884744 | tf_op jit(solution)/shard_map/ppermute | solution.py:275
  56.3 19.8 %collective-permute-start.19 = (bf16[3,384,128]{2,1,0:T(8,128)(2,1)}, bf16[3,384,128]{2,1,0:T(8,128)(2,1)S(1)}, u32[]{:S(2)}, u32[]{:S(2)}) collective-permute-start(bf16[3,384,128]{2,1,0:T(8,128)(2,1)} %collective-permute-done.18.refs_12_), channel_id=1, source_target_pairs={{0,1},{2,0},{4,2},{6,4},{7,6},{5,7},{3,5},{1,3},{8,9},{10,8},{12,1... | collective-permute-start | bytes 884744 | tf_op jit(solution)/shard_map/ppermute | solution.py:275
  60.7 8.6 %copy-start.16 = (bf16[128,1024]{1,0:T(8,128)(2,1)}, bf16[128,1024]{1,0:T(8,128)(2,1)S(1)}, u32[]{:S(2)}) copy-start(bf16[128,1024]{1,0:T(8,128)(2,1)S(1)} %collective-permute-done.2.refs_2_) | copy-start | bytes 786436
  60.7 8.6 %collective-permute-start.3 = (bf16[128,1024]{1,0:T(8,128)(2,1)}, bf16[128,1024]{1,0:T(8,128)(2,1)S(1)}, u32[]{:S(2)}, u32[]{:S(2)}) collective-permute-start(bf16[128,1024]{1,0:T(8,128)(2,1)} %get-tuple-element.36), channel_id=1, source_target_pairs={{0,24},{8,16},{16,8},{24,0},{1,25},{9,17},{17,9},{25,1},{2,26},{10... | collective-permute-start | bytes 786440 | tf_op jit(solution)/shard_map/ppermute | solution.py:328
  76.0 1.0 copy-start.14
  83.6 4.7 %copy-start.30 = (bf16[64,1152]{1,0:T(8,128)(2,1)S(1)}, bf16[64,1152]{1,0:T(8,128)(2,1)}, u32[]{:S(2)}) copy-start(bf16[64,1152]{1,0:T(8,128)(2,1)} %get-tuple-element.50) | copy-start | bytes 442372
  83.6 6.6 %copy-start.29 = (bf16[64,1152]{1,0:T(8,128)(2,1)S(1)}, bf16[64,1152]{1,0:T(8,128)(2,1)}, u32[]{:S(2)}) copy-start(bf16[64,1152]{1,0:T(8,128)(2,1)} %get-tuple-element.54) | copy-start | bytes 442372
  83.6 7.4 %copy-start.28 = (bf16[64,1152]{1,0:T(8,128)(2,1)S(1)}, bf16[64,1152]{1,0:T(8,128)(2,1)}, u32[]{:S(2)}) copy-start(bf16[64,1152]{1,0:T(8,128)(2,1)} %get-tuple-element.57) | copy-start | bytes 442372
  83.7 8.6 %copy-start.25 = (bf16[64,1152]{1,0:T(8,128)(2,1)S(1)}, bf16[64,1152]{1,0:T(8,128)(2,1)}, u32[]{:S(2)}) copy-start(bf16[64,1152]{1,0:T(8,128)(2,1)} %get-tuple-element.47) | copy-start | bytes 442372
  83.7 8.6 %collective-permute-start.21 = (bf16[64,1152]{1,0:T(8,128)(2,1)}, bf16[64,1152]{1,0:T(8,128)(2,1)S(1)}, u32[]{:S(2)}, u32[]{:S(2)}) collective-permute-start(bf16[64,1152]{1,0:T(8,128)(2,1)} %get-tuple-element.46), channel_id=1, source_target_pairs={{0,2},{2,4},{4,6},{6,7},{7,5},{5,3},{3,1},{1,0},{8,10},{10,12},{12... | collective-permute-start | bytes 442376 | tf_op jit(solution)/shard_map/ppermute | solution.py:287
  88.3 11.9 %copy-start.23 = (bf16[64,1152]{1,0:T(8,128)(2,1)S(1)}, bf16[64,1152]{1,0:T(8,128)(2,1)}, u32[]{:S(2)}) copy-start(bf16[64,1152]{1,0:T(8,128)(2,1)} %get-tuple-element.58) | copy-start | bytes 442372
  88.3 12.8 %copy-start.24 = (bf16[64,1152]{1,0:T(8,128)(2,1)S(1)}, bf16[64,1152]{1,0:T(8,128)(2,1)}, u32[]{:S(2)}) copy-start(bf16[64,1152]{1,0:T(8,128)(2,1)} %get-tuple-element.48) | copy-start | bytes 442372
  88.3 15.4 %copy-start.22 = (bf16[64,1152]{1,0:T(8,128)(2,1)S(1)}, bf16[64,1152]{1,0:T(8,128)(2,1)}, u32[]{:S(2)}) copy-start(bf16[64,1152]{1,0:T(8,128)(2,1)} %get-tuple-element.52) | copy-start | bytes 442372
  88.3 7.1 %collective-permute-start.25 = (bf16[64,1152]{1,0:T(8,128)(2,1)S(1)}, bf16[64,1152]{1,0:T(8,128)(2,1)S(1)}, u32[]{:S(2)}, u32[]{:S(2)}) collective-permute-start(bf16[64,1152]{1,0:T(8,128)(2,1)S(1)} %copy-done.30), channel_id=1, source_target_pairs={{0,1},{2,0},{4,2},{6,4},{7,6},{5,7},{3,5},{1,3},{8,9},{10,8},{12,1... | collective-permute-start | bytes 442376 | tf_op jit(solution)/shard_map/ppermute | solution.py:287
  90.3 7.7 %collective-permute-start.28 = (bf16[64,1152]{1,0:T(8,128)(2,1)S(1)}, bf16[64,1152]{1,0:T(8,128)(2,1)S(1)}, u32[]{:S(2)}, u32[]{:S(2)}) collective-permute-start(bf16[64,1152]{1,0:T(8,128)(2,1)S(1)} %copy-done.29), channel_id=1, source_target_pairs={{0,2},{2,4},{4,6},{6,7},{7,5},{5,3},{3,1},{1,0},{8,10},{10,12},{12... | collective-permute-start | bytes 442376 | tf_op jit(solution)/shard_map/ppermute | solution.py:287
  91.0 9.1 %collective-permute-start.31 = (bf16[64,1152]{1,0:T(8,128)(2,1)S(1)}, bf16[64,1152]{1,0:T(8,128)(2,1)S(1)}, u32[]{:S(2)}, u32[]{:S(2)}) collective-permute-start(bf16[64,1152]{1,0:T(8,128)(2,1)S(1)} %copy-done.28), channel_id=1, source_target_pairs={{0,1},{2,0},{4,2},{6,4},{7,6},{5,7},{3,5},{1,3},{8,9},{10,8},{12,1... | collective-permute-start | bytes 442376 | tf_op jit(solution)/shard_map/ppermute | solution.py:287
  92.3 12.5 %copy-start.21 = (bf16[64,1152]{1,0:T(8,128)(2,1)S(1)}, bf16[64,1152]{1,0:T(8,128)(2,1)}, u32[]{:S(2)}) copy-start(bf16[64,1152]{1,0:T(8,128)(2,1)} %get-tuple-element.56) | copy-start | bytes 442372
  92.4 8.8 %collective-permute-start.22 = (bf16[64,1152]{1,0:T(8,128)(2,1)S(1)}, bf16[64,1152]{1,0:T(8,128)(2,1)S(1)}, u32[]{:S(2)}, u32[]{:S(2)}) collective-permute-start(bf16[64,1152]{1,0:T(8,128)(2,1)S(1)} %add_convert_fusion.9), channel_id=1, source_target_pairs={{0,2},{2,4},{4,6},{6,7},{7,5},{5,3},{3,1},{1,0},{8,10},{10,12},{12... | collective-permute-start | bytes 442376 | tf_op jit(solution)/shard_map/ppermute | solution.py:287
  96.4 10.6 %copy-start.20 = (bf16[64,1152]{1,0:T(8,128)(2,1)S(1)}, bf16[64,1152]{1,0:T(8,128)(2,1)}, u32[]{:S(2)}) copy-start(bf16[64,1152]{1,0:T(8,128)(2,1)} %get-tuple-element.59) | copy-start | bytes 442372
  96.4 7.3 %collective-permute-start.26 = (bf16[64,1152]{1,0:T(8,128)(2,1)S(1)}, bf16[64,1152]{1,0:T(8,128)(2,1)S(1)}, u32[]{:S(2)}, u32[]{:S(2)}) collective-permute-start(bf16[64,1152]{1,0:T(8,128)(2,1)S(1)} %add_convert_fusion.6), channel_id=1, source_target_pairs={{0,1},{2,0},{4,2},{6,4},{7,6},{5,7},{3,5},{1,3},{8,9},{10,8},{12,1... | collective-permute-start | bytes 442376 | tf_op jit(solution)/shard_map/ppermute | solution.py:287
  99.0 8.9 %copy-start.19 = (bf16[64,1152]{1,0:T(8,128)(2,1)S(1)}, bf16[64,1152]{1,0:T(8,128)(2,1)}, u32[]{:S(2)}) copy-start(bf16[64,1152]{1,0:T(8,128)(2,1)} %get-tuple-element.49) | copy-start | bytes 442372
  99.0 5.9 %collective-permute-start.29 = (bf16[64,1152]{1,0:T(8,128)(2,1)S(1)}, bf16[64,1152]{1,0:T(8,128)(2,1)S(1)}, u32[]{:S(2)}, u32[]{:S(2)}) collective-permute-start(bf16[64,1152]{1,0:T(8,128)(2,1)S(1)} %add_convert_fusion.4), channel_id=1, source_target_pairs={{0,2},{2,4},{4,6},{6,7},{7,5},{5,3},{3,1},{1,0},{8,10},{10,12},{12... | collective-permute-start | bytes 442376 | tf_op jit(solution)/shard_map/ppermute | solution.py:287
  100.2 12.0 %copy-start.18 = (bf16[64,1152]{1,0:T(8,128)(2,1)S(1)}, bf16[64,1152]{1,0:T(8,128)(2,1)}, u32[]{:S(2)}) copy-start(bf16[64,1152]{1,0:T(8,128)(2,1)} %get-tuple-element.60) | copy-start | bytes 442372
  100.2 6.8 %collective-permute-start.32 = (bf16[64,1152]{1,0:T(8,128)(2,1)S(1)}, bf16[64,1152]{1,0:T(8,128)(2,1)S(1)}, u32[]{:S(2)}, u32[]{:S(2)}) collective-permute-start(bf16[64,1152]{1,0:T(8,128)(2,1)S(1)} %add_convert_fusion.2), channel_id=1, source_target_pairs={{0,1},{2,0},{4,2},{6,4},{7,6},{5,7},{3,5},{1,3},{8,9},{10,8},{12,1... | collective-permute-start | bytes 442376 | tf_op jit(solution)/shard_map/ppermute | solution.py:287
  101.2 11.9 %copy-start.27 = (bf16[64,1152]{1,0:T(8,128)(2,1)S(1)}, bf16[64,1152]{1,0:T(8,128)(2,1)}, u32[]{:S(2)}) copy-start(bf16[64,1152]{1,0:T(8,128)(2,1)} %get-tuple-element.45) | copy-start | bytes 442372
  101.2 6.6 %collective-permute-start.23 = (bf16[64,1152]{1,0:T(8,128)(2,1)S(1)}, bf16[64,1152]{1,0:T(8,128)(2,1)S(1)}, u32[]{:S(2)}, u32[]{:S(2)}) collective-permute-start(bf16[64,1152]{1,0:T(8,128)(2,1)S(1)} %add_convert_fusion.8), channel_id=1, source_target_pairs={{0,2},{2,4},{4,6},{6,7},{7,5},{5,3},{3,1},{1,0},{8,10},{10,12},{12... | collective-permute-start | bytes 442376 | tf_op jit(solution)/shard_map/ppermute | solution.py:287
  103.8 9.1 %collective-permute-start.27 = (bf16[64,1152]{1,0:T(8,128)(2,1)S(1)}, bf16[64,1152]{1,0:T(8,128)(2,1)S(1)}, u32[]{:S(2)}, u32[]{:S(2)}) collective-permute-start(bf16[64,1152]{1,0:T(8,128)(2,1)S(1)} %add_convert_fusion.5), channel_id=1, source_target_pairs={{0,1},{2,0},{4,2},{6,4},{7,6},{5,7},{3,5},{1,3},{8,9},{10,8},{12,1... | collective-permute-start | bytes 442376 | tf_op jit(solution)/shard_map/ppermute | solution.py:287
  104.8 12.8 %copy-start.26 = (bf16[64,1152]{1,0:T(8,128)(2,1)S(1)}, bf16[64,1152]{1,0:T(8,128)(2,1)}, u32[]{:S(2)}) copy-start(bf16[64,1152]{1,0:T(8,128)(2,1)} %get-tuple-element.53) | copy-start | bytes 442372
  104.9 8.3 %collective-permute-start.30 = (bf16[64,1152]{1,0:T(8,128)(2,1)S(1)}, bf16[64,1152]{1,0:T(8,128)(2,1)S(1)}, u32[]{:S(2)}, u32[]{:S(2)}) collective-permute-start(bf16[64,1152]{1,0:T(8,128)(2,1)S(1)} %add_convert_fusion.3), channel_id=1, source_target_pairs={{0,2},{2,4},{4,6},{6,7},{7,5},{5,3},{3,1},{1,0},{8,10},{10,12},{12... | collective-permute-start | bytes 442376 | tf_op jit(solution)/shard_map/ppermute | solution.py:287
  107.1 5.2 %collective-permute-start.33 = (bf16[64,1152]{1,0:T(8,128)(2,1)S(1)}, bf16[64,1152]{1,0:T(8,128)(2,1)S(1)}, u32[]{:S(2)}, u32[]{:S(2)}) collective-permute-start(bf16[64,1152]{1,0:T(8,128)(2,1)S(1)} %add_convert_fusion.1), channel_id=1, source_target_pairs={{0,1},{2,0},{4,2},{6,4},{7,6},{5,7},{3,5},{1,3},{8,9},{10,8},{12,1... | collective-permute-start | bytes 442376 | tf_op jit(solution)/shard_map/ppermute | solution.py:287
  107.9 5.2 %collective-permute-start.24 = (bf16[64,1152]{1,0:T(8,128)(2,1)S(1)}, bf16[64,1152]{1,0:T(8,128)(2,1)S(1)}, u32[]{:S(2)}, u32[]{:S(2)}) collective-permute-start(bf16[64,1152]{1,0:T(8,128)(2,1)S(1)} %add_convert_fusion.7), channel_id=1, source_target_pairs={{0,2},{2,4},{4,6},{6,7},{7,5},{5,3},{3,1},{1,0},{8,10},{10,12},{12... | collective-permute-start | bytes 442376 | tf_op jit(solution)/shard_map/ppermute | solution.py:287
  112.3 5.3 %collective-permute-start.34 = (bf16[64,1152]{1,0:T(8,128)(2,1)S(1)}, bf16[64,1152]{1,0:T(8,128)(2,1)S(1)}, u32[]{:S(2)}, u32[]{:S(2)}) collective-permute-start(bf16[64,1152]{1,0:T(8,128)(2,1)S(1)} %add_convert_fusion), channel_id=1, source_target_pairs={{0,1},{2,0},{4,2},{6,4},{7,6},{5,7},{3,5},{1,3},{8,9},{10,8},{12,1... | collective-permute-start | bytes 442376 | tf_op jit(solution)/shard_map/ppermute | solution.py:287
  (4 other events, 3.2 us)
where the time goes:
time: 121 us; the launch traced here: 119 us
  waiting for transfers between devices  42.9 us (35%)
  starting transfers between devices  40.1 us (33%)
  Pallas kernels  30.2 us (25%)
  local copies, waits for them, and re-layouts  3.09 us (3%)
  other arithmetic  2.4 us (2%)
    ppermute x14, starting transfers between devices, cycle_gather(): moving = lax.ppermute(moving, 'seq', ring_pairs(size, -way))  16.9 us
    ppermute x6, waiting for transfers between devices, exchange(): got.append(lax.ppermute(messages[step], 'grp', pairs))  16.5 us
    ppermute x14, starting transfers between devices, cycle_reduce(): moving = lax.ppermute(moving, 'seq', ring_pairs(size, way))  15.9 us
    ppermute x14, waiting for transfers between devices, cycle_reduce(): moving = lax.ppermute(moving, 'seq', ring_pairs(size, way))  11.1 us
    ppermute x14, waiting for transfers between devices, cycle_gather(): moving = lax.ppermute(moving, 'seq', ring_pairs(size, -way))  8.13 us
    ppermute x1, waiting for transfers between devices, body(): rim = lax.ppermute(edge, 'seq', [(i, i + 1) for i in range(size - 1)])  7.12 us
    pallas_call x1, Pallas kernels, body(): kernel(functools.partial(gate_kernel, groups, near, far, size, length, in...  6.59 us
    pallas_call x1, Pallas kernels, body(): kernel(functools.partial(first_kernel, groups, near, far, size, length),...  5.93 us
  transfers between devices with their start and end apart: 35, of which 12 were waited for; matrix products, arithmetic and copies ran while one was open for 2% of the time, Pallas kernels for 18%

commit v1 on v0

v1 whole, which is shorter than its diff:
```python
import functools
import math

import jax
import jax.numpy as jnp
from jax import lax
from jax.experimental import pallas as pl
from jax.experimental.pallas import tpu as pltpu
from jax.sharding import PartitionSpec as P


HD = 64
WINDOW = 256
EPSILON = 1e-05
TILE = 128
LANES = 128
MARK = 16
NEG = -1e30
GRANT = 24 * 2**20


VMEM = pl.BlockSpec(memory_space=pltpu.VMEM)
SMEM = pl.BlockSpec(memory_space=pltpu.SMEM)


def ring_order(size):
    return list(range(0, size, 2)) + [i for i in range(size - 1, 0, -1) if i % 2]


def ring_pairs(size, step):
    order = ring_order(size)
    return [(order[i], order[(i + step) % size]) for i in range(size)]


def ring_place(index, size):
    half = index // 2
    return jnp.where(index % 2 == 0, half, size - 1 - half)


def ring_member(place, size):
    place = jnp.where(place >= size, place - size, place)
    ups = (size + 1) // 2
    return jnp.where(place < ups, 2 * place, 2 * (size - place) - 1)


def peer_of(index, step, size):
    if size & (size - 1) == 0:
        return index ^ step
    return (index + step) % size


def dot(a, b, dims):
    return lax.dot_general(a, b, (dims, ((), ())), preferred_element_type=jnp.float32)


def attend(q_ref, q_row, k_win, v_win, ctx_ref, row0, bias):
    width = q_ref.shape[1]
    group = min(width, 256)
    heads = group // HD
    for col0 in range(0, width, group):
        q_part = q_ref[q_row : q_row + TILE, col0 : col0 + group] * jnp.bfloat16(HD**-0.5)
        lane_head = lax.broadcasted_iota(jnp.int32, q_part.shape, 1) // HD
        q_diag = jnp.concatenate(
            [jnp.where(lane_head == h, q_part, jnp.zeros_like(q_part)) for h in range(heads)], axis=0
        )
        keys = k_win[:, col0 : col0 + group]
        vals = v_win[:, col0 : col0 + group]
        scores = dot(q_diag, keys, ((1,), (1,)))
        scores = scores.reshape(heads, TILE, scores.shape[1]) + bias[None]
        weights = jnp.exp(scores - jnp.max(scores, axis=-1, keepdims=True))
        inverse = 1.0 / jnp.sum(weights, axis=-1, keepdims=True)
        weights = weights.astype(jnp.bfloat16).reshape(heads * TILE, -1)
        mixed = dot(weights, vals, ((1,), (0,)))
        picked = jnp.zeros((TILE, group), jnp.float32)
        for h in range(heads):
            one = mixed[h * TILE : (h + 1) * TILE] * inverse[h]
            picked = jnp.where(lane_head == h, one, picked)
        ctx_ref[row0 : row0 + TILE, col0 : col0 + group] = picked.astype(jnp.bfloat16)


def window_bias():
    shape = (TILE, TILE + WINDOW)
    row = lax.broadcasted_iota(jnp.int32, shape, 0)
    col = lax.broadcasted_iota(jnp.int32, shape, 1)
    allowed = (col <= row + WINDOW) & (col > row)
    return jnp.where(allowed, 0.0, NEG).astype(jnp.float32), col


def finish_rows(ctx_ref, resid, wo_ref):
    hidden = (
        resid.astype(jnp.float32) + dot(ctx_ref[...], wo_ref[...], ((1,), (0,)))
    ).astype(jnp.bfloat16).astype(jnp.float32)
    center = hidden - jnp.mean(hidden, axis=-1, keepdims=True)
    spread = jnp.mean(center * center, axis=-1, keepdims=True)
    return (center * lax.rsqrt(spread + EPSILON)).astype(jnp.bfloat16)


def late_kernel(q_ref, k_ref, v_ref, r_ref, wo_ref, out_ref, ctx_ref):
    bias, _ = window_bias()
    for row0 in range(0, ctx_ref.shape[0], TILE):
        span = slice(row0, row0 + TILE + WINDOW)
        attend(q_ref, WINDOW + row0, k_ref[span, :], v_ref[span, :], ctx_ref, row0, bias)
    out_ref[...] = finish_rows(ctx_ref, r_ref[WINDOW:, :], wo_ref)


def block_for(lang_ref, owner, rank, lang_grp):
    block, local, seen = jnp.int32(0), jnp.int32(-1), jnp.int32(0)
    for b in range(lang_ref.shape[0]):
        lang = lang_ref[b]
        mine = (lang >= owner * lang_grp) & (lang < (owner + 1) * lang_grp)
        take = mine & (seen == rank)
        block = jnp.where(take, b, block)
        local = jnp.where(take, lang - owner * lang_grp, local)
        seen = seen + mine.astype(jnp.int32)
    return block, local


def early_kernel(
    groups, lang_grp, lang_ref, q_ref, rim_ref, k_ref, v_ref, r_ref, wo_ref, late_ref, *rest
):
    outs, (ctx_ref, kk_ref, vv_ref, rows_ref) = rest[:groups], rest[groups:]
    rows = WINDOW
    width = q_ref.shape[1]
    kk_ref[:WINDOW, :] = rim_ref[:, :width]
    vv_ref[:WINDOW, :] = rim_ref[:, width:]
    kk_ref[WINDOW:, :] = k_ref[:WINDOW, :]
    vv_ref[WINDOW:, :] = v_ref[:WINDOW, :]
    bias, col = window_bias()
    first = lax.axis_index("seq") == 0
    for row0 in range(0, rows, TILE):
        span = slice(row0, row0 + TILE + WINDOW)
        shut = jnp.logical_and(first, col + row0 < WINDOW)
        mask = jnp.where(shut, NEG, bias)
        attend(q_ref, row0, kk_ref[span, :], vv_ref[span, :], ctx_ref, row0, mask)
    blocks = lang_ref.shape[0]
    length = rows_ref.shape[1]
    done = finish_rows(ctx_ref, r_ref[:rows, :], wo_ref)
    split = rows // length
    rows_ref[:split] = done.reshape(split, length, -1)
    rows_ref[split:] = late_ref[...].reshape(blocks - split, length, -1)
    me = lax.axis_index("grp")
    for step, out_ref in enumerate(outs):
        owner = peer_of(me, step, groups)
        for j in range(out_ref.shape[0] // length):
            block, _ = block_for(lang_ref, owner, j, lang_grp)
            out_ref[j * length : (j + 1) * length, :] = rows_ref[block]


def pack_kernel(groups, lang_grp, lang_ref, c_ref, *outs):
    length = c_ref.shape[1]
    me = lax.axis_index("grp")
    for step, out_ref in enumerate(outs):
        owner = peer_of(me, step, groups)
        cap = (out_ref.shape[0] - MARK) // length
        row = lax.broadcasted_iota(jnp.int32, (MARK, out_ref.shape[1]), 0)
        mark = jnp.full(row.shape, -1.0, jnp.float32)
        for j in range(cap):
            block, local = block_for(lang_ref, owner, j, lang_grp)
            out_ref[j * length : (j + 1) * length, :] = c_ref[block]
            mark = jnp.where(row == j, local.astype(jnp.float32), mark)
        out_ref[cap * length :, :] = mark.astype(jnp.bfloat16)


def gelu_slope(v):
    rate = math.sqrt(2 / math.pi)
    square = v * v
    t = jnp.tanh(rate * v * (1.0 + 0.044715 * square))
    return 0.5 * (1.0 + t) + (0.5 * rate) * v * (1.0 - t * t) * (1.0 + (3 * 0.044715) * square)


def project(x, cot, downs, ups):
    lang_grp, width, units = downs[0].shape
    w_down = jnp.concatenate(
        [jnp.concatenate([d[l] for l in range(lang_grp)], axis=1) for d in downs], axis=0
    )
    w_up = jnp.concatenate([u[...].reshape(lang_grp * units, width) for u in ups], axis=1)
    return dot(x, w_down, ((1,), (0,))), dot(cot, w_up, ((1,), (1,)))


def of_language(table, lang, units):
    value = table[:, :units]
    for l in range(1, table.shape[1] // units):
        value = jnp.where(lang == l, table[:, l * units : (l + 1) * units], value)
    return value


def by_offset(refs, offsets, size, width, to_ref):
    place = ring_place(lax.axis_index("seq"), size)
    part = to_ref.shape[0] // len(refs)
    for at, k in enumerate(offsets):
        member = ring_member(place + k, size)
        columns = pl.ds(pl.multiple_of(member * width, width), width)
        for i, ref in enumerate(refs):
            to_ref[i * part : (i + 1) * part, at * width : (at + 1) * width] = ref[:part, columns]


def first_kernel(groups, near, far, size, length, *refs):
    refs = list(refs)
    take = lambda count: [refs.pop(0) for _ in range(count)]
    rows, cots = take(groups), take(groups)
    chunks = max(1, len(near))
    downs, ups = take(chunks), take(chunks)
    (bias_ref,) = take(1)
    turned_ref, pre_ref, back_ref, mark_ref = take(4)
    lang_grp, width, units = downs[0].shape
    part = rows[0].shape[0]
    if near:
        xf_ref, cf_ref, x_ref, c_ref = refs
        by_offset(rows, near, size, width, x_ref)
        by_offset(rows, far, size, width, xf_ref)
        by_offset(cots, near, size, width, c_ref)
        by_offset(cots, far, size, width, cf_ref)
        turned_ref[x_ref.shape[1] :, :] = xf_ref[...].T
    else:
        x_ref, c_ref = refs
        for i in range(groups):
            x_ref[i * part : (i + 1) * part, :] = rows[i][...]
            c_ref[i * part : (i + 1) * part, :] = cots[i][:part, :]
    turned_ref[: x_ref.shape[1], :] = x_ref[...].T
    pre, back = project(x_ref[...], c_ref[...], downs, ups)
    cap = part // length
    for i, ref in enumerate(cots):
        for j in range(cap):
            at = i * cap + j
            lang = ref[part:, :units].astype(jnp.float32)[j : j + 1, :]
            mark_ref[at : at + 1, :] = lang
            bias = bias_ref[0:1, :]
            for l in range(1, lang_grp):
                bias = jnp.where(lang == l, bias_ref[l : l + 1, :], bias)
            span = slice(at * length, (at + 1) * length)
            pre_ref[span, :] = of_language(pre[span], lang, units) + bias
            back_ref[span, :] = of_language(back[span], lang, units)


def gate_kernel(near, far, length, inv_scale, *refs):
    refs = list(refs)
    take = lambda count: [refs.pop(0) for _ in range(count)]
    turned_ref, pre_ref, back_ref, mark_ref = take(4)
    tokens, units = pre_ref.shape
    if far:
        xf_ref, cf_ref = take(2)
        downs, ups = take(len(far)), take(len(far))
        pre, back = project(xf_ref[...], cf_ref[...], downs, ups)
    g_ref = refs.pop(0)
    for j in range(tokens // length):
        span = slice(j * length, (j + 1) * length)
        lang = mark_ref[j : j + 1, :]
        value, other = pre_ref[span, :], back_ref[span, :]
        if far:
            value = value + of_language(pre[span], lang, units)
            other = other + of_language(back[span], lang, units)
        gate = (gelu_slope(value) * other).astype(jnp.bfloat16)
        for l in range(g_ref.shape[1] // units):
            g_ref[span, l * units : (l + 1) * units] = jnp.where(
                lang == l, gate, jnp.zeros_like(gate)
            )
    if far:
        slabs(turned_ref, len(near), g_ref, refs, inv_scale)


def slabs(turned_ref, skip, g_ref, outs, inv_scale):
    count = outs[0].shape[0]
    for i in range(0, len(outs), 2):
        at = (2 * skip + i) * count
        pair = outs[i : i + 2]
        slab = dot(turned_ref[at : at + len(pair) * count, :], g_ref[...], ((1,), (0,)))
        slab = (slab * inv_scale).astype(jnp.bfloat16)
        for h, out_ref in enumerate(pair):
            out_ref[...] = slab[h * count : (h + 1) * count]


def slab_kernel(inv_scale, turned_ref, g_ref, *outs):
    slabs(turned_ref, 0, g_ref, outs, inv_scale)


def close_kernel(*refs):
    out_ref = refs[-1]
    lang_grp, share, units = out_ref.shape
    count = share // 2
    for h in range(2):
        terms = [ref[...].astype(jnp.float32) for ref in refs[3 * h : 3 * h + 3]]
        total = terms[0] + terms[1] + terms[2]
        for l in range(lang_grp):
            out_ref[l, h * count : (h + 1) * count, :] = total[:, l * units : (l + 1) * units]


def cycle_gather(value, size, far):
    held = {0: value}
    half = size // 2
    for way in (-1, 1):
        moving = value
        for hop in range(1, half + (1 if way == far else 0)):
            moving = lax.ppermute(moving, "seq", ring_pairs(size, -way))
            held[(way * hop) % size] = moving
    return [held[k] for k in range(size)]


def cycle_reduce(parts, size, far):
    half = size // 2
    found = [parts[0]]
    for way in (1, -1):
        hops = half if way == far else half - 1
        moving = parts[(way * hops) % size]
        for hop in range(hops - 1, -1, -1):
            moving = lax.ppermute(moving, "seq", ring_pairs(size, way))
            if hop:
                mine = parts[(way * hop) % size]
                moving = (moving.astype(jnp.float32) + mine.astype(jnp.float32)).astype(mine.dtype)
        found.append(moving)
    return found


def kernel(fn, args, outs, scratch=(), final=False):
    small = [a.dtype == jnp.int32 for a in args]
    placed = [
        a if s else pltpu.with_memory_space_constraint(a, pltpu.VMEM) for a, s in zip(args, small)
    ]
    make = jax.ShapeDtypeStruct if final else pltpu.VMEM
    return pl.pallas_call(
        fn,
        out_shape=[make(shape, dtype) for shape, dtype in outs],
        in_specs=[SMEM if s else VMEM for s in small],
        out_specs=[VMEM] * len(outs),
        scratch_shapes=[pltpu.VMEM(shape, dtype) for shape, dtype in scratch],
        compiler_params=pltpu.CompilerParams(vmem_limit_bytes=GRANT),
    )(*placed)


def body(queries, keys, values, resid, w_out, block_lang, w_down, w_up, bias_down, cotangent):
    tok_dev, width_q = queries.shape
    model = resid.shape[1]
    blocks = block_lang.shape[0]
    length = tok_dev // blocks
    groups = lax.axis_size("grp")
    size = lax.axis_size("seq")
    cap = max(1, blocks // groups)
    lang_grp, _, units = w_down.shape
    bf16 = jnp.bfloat16
    late = tok_dev - WINDOW

    edge = jnp.concatenate([keys[late:], values[late:]], axis=1)
    rim = lax.ppermute(edge, "seq", [(i, i + 1) for i in range(size - 1)])

    downs = cycle_gather(w_down, size, -1)
    ups = cycle_gather(w_up, size, 1)

    cot_out = kernel(
        functools.partial(pack_kernel, groups, lang_grp),
        [block_lang, cotangent.reshape(blocks, length, model)],
        [((cap * length + MARK, model), bf16)] * groups,
    )

    def exchange(messages):
        got = [messages[0]]
        for step in range(1, groups):
            pairs = [(i, peer_of(i, step, groups)) for i in range(groups)]
            got.append(lax.ppermute(messages[step], "grp", pairs))
        return got

    cots = exchange(cot_out)

    (rows_late,) = kernel(
        late_kernel,
        [queries, keys, values, resid, w_out],
        [((late, model), bf16)],
        [((late, width_q), bf16)],
    )
    row_out = kernel(
        functools.partial(early_kernel, groups, lang_grp),
        [block_lang, queries, rim, keys, values, resid, w_out, rows_late],
        [((cap * length, model), bf16)] * groups,
        [
            ((WINDOW, width_q), bf16),
            ((2 * WINDOW, width_q), bf16),
            ((2 * WINDOW, width_q), bf16),
            ((blocks, length, model), bf16),
        ],
    )
    rows = exchange(row_out)

    share = model // size
    whole = share % LANES != 0
    cells = lang_grp * units
    half = size // 2
    near, far = [], []
    if whole:
        place = ring_place(lax.axis_index("seq"), size)
        at_offset = ring_member(place + jnp.arange(size), size)
        of_member = jnp.argsort(at_offset)
        stack = jnp.take(jnp.stack(downs), of_member, axis=0)
        downs = [stack.transpose(1, 0, 2, 3).reshape(lang_grp, model, units)]
        stack = jnp.take(jnp.stack(ups), of_member, axis=0)
        ups = [stack.transpose(1, 2, 0, 3).reshape(lang_grp, units, model)]
        downs_near, ups_near, downs_far, ups_far = downs, ups, [], []
        far_rows, near_rows = [], [model]
        near_width = model
    else:
        far = [half, half - 1, half + 1]
        near = [k for k in range(size) if k not in far]
        pick = lambda held, offsets: [held[k] for k in offsets]
        downs_near, ups_near = pick(downs, near), pick(ups, near)
        downs_far, ups_far = pick(downs, far), pick(ups, far)
        far_rows, near_rows = [share // 2] * (2 * len(far)), [share // 2] * (2 * len(near))
        near_width = share * len(near)
    tokens = groups * cap * length
    far_width = share * len(far)
    f32 = jnp.float32
    spare = [((tokens, far_width), bf16)] * 2 if far else []
    turned, pre, back, marks, *far_x = kernel(
        functools.partial(first_kernel, groups, near, far, size, length),
        [*rows, *cots, *downs_near, *ups_near, bias_down.astype(f32)],
        [
            ((model, tokens), bf16),
            ((tokens, units), f32),
            ((tokens, units), f32),
            ((tokens // length, units), f32),
        ]
        + spare,
        [((tokens, near_width), bf16)] * 2,
    )
    inv_scale = 1.0 / math.sqrt(tok_dev * size)
    gate, *far_slabs = kernel(
        functools.partial(gate_kernel, near, far, length, inv_scale),
        [turned, pre, back, marks, *far_x, *downs_far, *ups_far],
        [((tokens, cells), bf16)] + [((c, cells), bf16) for c in far_rows],
    )
    near_slabs = kernel(
        functools.partial(slab_kernel, inv_scale),
        [turned, gate],
        [((c, cells), bf16) for c in near_rows],
    )
    if whole:
        cut = jnp.take(near_slabs[0].reshape(size, 2, share // 2, cells), at_offset, axis=0)
        parts = [[cut[k, h] for k in range(size)] for h in range(2)]
    else:
        parts = []
        for h in range(2):
            found = dict(zip(near, near_slabs[h::2])) | dict(zip(far, far_slabs[h::2]))
            parts.append([found[k] for k in range(size)])
    upper = cycle_reduce(parts[0], size, 1)
    lower = cycle_reduce(parts[1], size, -1)
    (total,) = kernel(close_kernel, [*upper, *lower], [((lang_grp, share, units), f32)], final=True)
    return total.transpose(1, 0, 2)


def solution(mesh):
    in_specs = (
        P(("grp", "seq"), None),
        P(("grp", "seq"), None),
        P(("grp", "seq"), None),
        P(("grp", "seq"), None),
        P(),
        P(("grp", "seq")),
        P("grp", "seq", None),
        P("grp", None, "seq"),
        P("grp", None),
        P(("grp", "seq"), None),
    )
    out_specs = P("seq", "grp", None)

    return jax.shard_map(body, mesh=mesh, in_specs=in_specs, out_specs=out_specs, check_vma=False)
```

time: 121 us -> 102 us (0.84); the launches traced: 119 us -> 101 us
  Pallas kernels: 30.2 us -> 12.4 us
  waiting for transfers between devices: 42.9 us -> 45.3 us
  other arithmetic: 2.4 us -> 0.43 us
  starting transfers between devices: 40.1 us -> 38.8 us
    pallas_call x6 -> x7, Pallas kernels: 30.2 us -> 12.4 us  [kernel(): pl.pallas_call(fn, out_shape=[make(shape, dtype) for shape, dtype in outs...]
    ppermute x14, waiting for transfers between devices: 11.1 us -> 13.8 us  [cycle_reduce(): moving = lax.ppermute(moving, 'seq', ring_pairs(size, way))]
    unnamed x62 -> x22, local copies, waits for them, and re-layouts: 1.8 us -> 4.05 us
    convert_element_type x10, other arithmetic: 2.2 us -> 0.38 us  [cycle_reduce(): (moving.astype(jnp.float32) + mine.astype(jnp.float32)).astype(mine.dtype)]
    ppermute x14, starting transfers between devices: 15.9 us -> 14.7 us  [cycle_reduce(): moving = lax.ppermute(moving, 'seq', ring_pairs(size, way))]
  transfers between devices with their start and end apart: 35 -> 35, of which waited for: 12 -> 15; matrix products, arithmetic and copies ran while one was open for 2% -> 0% of each run, Pallas kernels for 18% -> 8%
where the time goes in v1:
time: 102 us; the launch traced here: 101 us
  waiting for transfers between devices  45.3 us (44%)
  starting transfers between devices  38.8 us (38%)
  Pallas kernels  12.4 us (12%)
  local copies, waits for them, and re-layouts  4.06 us (4%)
    ppermute x14, starting transfers between devices, cycle_gather(): moving = lax.ppermute(moving, 'seq', ring_pairs(size, -way))  16.7 us
    ppermute x6, waiting for transfers between devices, exchange(): got.append(lax.ppermute(messages[step], 'grp', pairs))  15.9 us
    ppermute x14, starting transfers between devices, cycle_reduce(): moving = lax.ppermute(moving, 'seq', ring_pairs(size, way))  14.7 us
    ppermute x14, waiting for transfers between devices, cycle_reduce(): moving = lax.ppermute(moving, 'seq', ring_pairs(size, way))  13.8 us
    pallas_call x7, Pallas kernels, kernel(): pl.pallas_call(fn, out_shape=[make(shape, dtype) for shape, dtype in outs...  12.4 us
    ppermute x14, waiting for transfers between devices, cycle_gather(): moving = lax.ppermute(moving, 'seq', ring_pairs(size, -way))  8.41 us
    ppermute x1, waiting for transfers between devices, body(): rim = lax.ppermute(edge, 'seq', [(i, i + 1) for i in range(size - 1)])  7.21 us
    unnamed x22, local copies, waits for them, and re-layouts  4.05 us
  transfers between devices with their start and end apart: 35, of which 15 were waited for; matrix products, arithmetic and copies ran while one was open for 0% of the time, Pallas kernels for 8%

profile of v1, /device:TPU:0, one launch (start us, length us, event | category | flops | bytes accessed | tf_op | source)
XLA Modules:
  0.0 101.3 jit_solution(5864851689733397549)
XLA Ops:
  0.0 1.3 %copy-done.5 = bf16[512,1024]{1,0:T(8,128)(2,1)S(1)} copy-done((bf16[512,1024]{1,0:T(8,128)(2,1)S(1)}, bf16[512,1024]{1,0:T(8,128)(2,1)}, u32[]{:S(2)}) %copy-start.5) | copy-done | bytes 1048600
  1.3 0.7 copy-done.8
  1.9 0.8 shard_map.102
  2.7 0.0 copy-start
  2.7 0.0 copy-start.1
  2.7 0.6 collective-permute-start.4
  3.3 2.6 %collective-permute-start.5 = (bf16[144,1024]{1,0:T(8,128)(2,1)S(1)}, bf16[144,1024]{1,0:T(8,128)(2,1)S(1)}, u32[]{:S(2)}, u32[]{:S(2)}) collective-permute-start(bf16[144,1024]{1,0:T(8,128)(2,1)S(1)} %get-tuple-element.42), channel_id=1, source_target_pairs={{0,16},{8,24},{16,0},{24,8},{1,17},{9,25},{17,1},{25,9},{2,18},{10... | collective-permute-start | bytes 884744 | tf_op jit(solution)/shard_map/ppermute | solution.py:357
  5.9 1.5 %collective-permute-start.11 = (bf16[3,384,128]{2,1,0:T(8,128)(2,1)}, bf16[3,384,128]{2,1,0:T(8,128)(2,1)S(1)}, u32[]{:S(2)}, u32[]{:S(2)}) collective-permute-start(bf16[3,384,128]{2,1,0:T(8,128)(2,1)} %refs_13_.1), channel_id=1, source_target_pairs={{0,1},{2,0},{4,2},{6,4},{7,6},{5,7},{3,5},{1,3},{8,9},{10,8},{12,1... | collective-permute-start | bytes 884744 | tf_op jit(solution)/shard_map/ppermute | solution.py:293
  7.4 0.5 collective-permute-start.13
  7.9 1.6 %collective-permute-start.9 = (bf16[3,128,384]{2,1,0:T(8,128)(2,1)}, bf16[3,128,384]{2,1,0:T(8,128)(2,1)S(1)}, u32[]{:S(2)}, u32[]{:S(2)}) collective-permute-start(bf16[3,128,384]{2,1,0:T(8,128)(2,1)} %refs_8_.1), channel_id=1, source_target_pairs={{0,2},{2,4},{4,6},{6,7},{7,5},{5,3},{3,1},{1,0},{8,10},{10,12},{12... | collective-permute-start | bytes 884744 | tf_op jit(solution)/shard_map/ppermute | solution.py:293
  9.5 0.5 collective-permute-start.7
  10.0 3.5 %collective-permute-done.5.refs_6_ = bf16[144,1024]{1,0:T(8,128)(2,1)S(1)} collective-permute-done((bf16[144,1024]{1,0:T(8,128)(2,1)S(1)}, bf16[144,1024]{1,0:T(8,128)(2,1)S(1)}, u32[]{:S(2)}, u32[]{:S(2)}) %collective-permute-start.5) | collective-permute-done | bytes 294944 | tf_op jit(solution)/shard_map/ppermute | solution.py:357
  13.5 3.6 %collective-permute-start = (bf16[256,1024]{1,0:T(8,128)(2,1)S(1)}, bf16[256,1024]{1,0:T(8,128)(2,1)S(1)}, u32[]{:S(2)}, u32[]{:S(2)}) collective-permute-start(bf16[256,1024]{1,0:T(8,128)(2,1)S(1)} %pad_maximum_fusion), channel_id=1, source_target_pairs={{0,1},{1,2},{2,3},{3,4},{4,5},{5,6},{6,7},{8,9},{9,10},{10,11},{11... | collective-permute-start | bytes 1572872 | tf_op jit(solution)/shard_map/ppermute | solution.py:342
  17.1 5.6 %collective-permute-done.9.refs_12_ = bf16[3,128,384]{2,1,0:T(8,128)(2,1)S(1)} collective-permute-done((bf16[3,128,384]{2,1,0:T(8,128)(2,1)}, bf16[3,128,384]{2,1,0:T(8,128)(2,1)S(1)}, u32[]{:S(2)}, u32[]{:S(2)}) %collective-permute-start.9) | collective-permute-done | bytes 294944 | tf_op jit(solution)/shard_map/ppermute | solution.py:293
  22.7 0.5 collective-permute-start.10
  23.2 1.5 %collective-permute-start.12 = (bf16[3,384,128]{2,1,0:T(8,128)(2,1)S(1)}, bf16[3,384,128]{2,1,0:T(8,128)(2,1)S(1)}, u32[]{:S(2)}, u32[]{:S(2)}) collective-permute-start(bf16[3,384,128]{2,1,0:T(8,128)(2,1)S(1)} %collective-permute-done.11.refs_14_), channel_id=1, source_target_pairs={{0,1},{2,0},{4,2},{6,4},{7,6},{5,7},{3,5},{1,3},{8,9},{10,8},{12,1... | collective-permute-start | bytes 884744 | tf_op jit(solution)/shard_map/ppermute | solution.py:293
  24.7 0.6 collective-permute-start.14
  25.3 7.2 %collective-permute-done.rim_ref = bf16[256,1024]{1,0:T(8,128)(2,1)S(1)} collective-permute-done((bf16[256,1024]{1,0:T(8,128)(2,1)S(1)}, bf16[256,1024]{1,0:T(8,128)(2,1)S(1)}, u32[]{:S(2)}, u32[]{:S(2)}) %collective-permute-start) | collective-permute-done | bytes 524320 | tf_op jit(solution)/shard_map/ppermute | solution.py:342
  32.5 2.5 %collective-permute-start.8 = (bf16[3,128,384]{2,1,0:T(8,128)(2,1)S(1)}, bf16[3,128,384]{2,1,0:T(8,128)(2,1)S(1)}, u32[]{:S(2)}, u32[]{:S(2)}) collective-permute-start(bf16[3,128,384]{2,1,0:T(8,128)(2,1)S(1)} %collective-permute-done.7.refs_9_), channel_id=1, source_target_pairs={{0,1},{2,0},{4,2},{6,4},{7,6},{5,7},{3,5},{1,3},{8,9},{10,8},{12,1... | collective-permute-start | bytes 884744 | tf_op jit(solution)/shard_map/ppermute | solution.py:293
  35.0 1.0 %collective-permute-start.15 = (bf16[3,128,384]{2,1,0:T(8,128)(2,1)S(1)}, bf16[3,128,384]{2,1,0:T(8,128)(2,1)S(1)}, u32[]{:S(2)}, u32[]{:S(2)}) collective-permute-start(bf16[3,128,384]{2,1,0:T(8,128)(2,1)S(1)} %collective-permute-done.10.refs_11_), channel_id=1, source_target_pairs={{0,2},{2,4},{4,6},{6,7},{7,5},{5,3},{3,1},{1,0},{8,10},{10,12},{12... | collective-permute-start | bytes 884744 | tf_op jit(solution)/shard_map/ppermute | solution.py:293
  36.0 2.8 %collective-permute-done.12.refs_15_ = bf16[3,384,128]{2,1,0:T(8,128)(2,1)S(1)} collective-permute-done((bf16[3,384,128]{2,1,0:T(8,128)(2,1)S(1)}, bf16[3,384,128]{2,1,0:T(8,128)(2,1)S(1)}, u32[]{:S(2)}, u32[]{:S(2)}) %collective-permute-start.12) | collective-permute-done | bytes 294944 | tf_op jit(solution)/shard_map/ppermute | solution.py:293
  38.8 2.5 %collective-permute-start.18 = (bf16[3,384,128]{2,1,0:T(8,128)(2,1)S(1)}, bf16[3,384,128]{2,1,0:T(8,128)(2,1)S(1)}, u32[]{:S(2)}, u32[]{:S(2)}) collective-permute-start(bf16[3,384,128]{2,1,0:T(8,128)(2,1)S(1)} %collective-permute-done.12.refs_15_), channel_id=1, source_target_pairs={{0,1},{2,0},{4,2},{6,4},{7,6},{5,7},{3,5},{1,3},{8,9},{10,8},{12,1... | collective-permute-start | bytes 884744 | tf_op jit(solution)/shard_map/ppermute | solution.py:293
  41.3 1.0 %copy-done.3 = bf16[512,512]{1,0:T(8,128)(2,1)S(1)} copy-done((bf16[512,512]{1,0:T(8,128)(2,1)S(1)}, bf16[512,512]{1,0:T(8,128)(2,1)}, u32[]{:S(2)}) %copy-start.3) | copy-done | bytes 524312
  42.4 1.0 %copy-done.4 = bf16[512,512]{1,0:T(8,128)(2,1)S(1)} copy-done((bf16[512,512]{1,0:T(8,128)(2,1)S(1)}, bf16[512,512]{1,0:T(8,128)(2,1)}, u32[]{:S(2)}) %copy-start.4) | copy-done | bytes 524312
  43.4 2.1 %shard_map.100.late_ref = bf16[256,1024]{1,0:T(8,128)(2,1)S(1)} custom-call(bf16[512,512]{1,0:T(8,128)(2,1)S(1)} %copy-done.4, bf16[512,512]{1,0:T(8,128)(2,1)S(1)} %copy-done.3, bf16[512,512]{1,0:T(8,128)(2,1)S(1)} %copy-done.2, bf16[512,1024]{1,0:T(8,128)(2,1)S(1)} %copy-done, bf16[512,1024]{1,0:T(8,128)(2,1)S(1)} %copy-done.1), custom_call_target="tpu_custom_call" | custom-call | tf_op jit(solution)/shard_map/pallas_call | solution.py:319
  45.6 0.0 copy-start.10
  45.6 0.0 copy-start.6
  45.6 0.0 copy-start.7
  45.6 2.8 %shard_map.101 = (bf16[128,1024]{1,0:T(8,128)(2,1)S(1)}, bf16[128,1024]{1,0:T(8,128)(2,1)S(1)}, bf16[128,1024]{1,0:T(8,128)(2,1)S(1)}, bf16[128,1024]{1,0:T(8,128)(2,1)S(1)}) custom-call(s32[8]{0:T(128)S(1)} %copy-done.9, bf16[512,512]{1,0:T(8,128)(2,1)S(1)} %copy-done.4, bf16[256,1024]{1,0:T(8,128)(2,1)S(1)} %collective-permute-done.rim_ref, ...), custom_call_target="tpu_custom_call" | custom-call | tf_op jit(solution)/shard_map/pallas_call | solution.py:319
  48.4 0.1 collective-permute-start.1
  48.5 0.6 collective-permute-start.2
  49.1 1.6 %collective-permute-start.17 = (bf16[3,128,384]{2,1,0:T(8,128)(2,1)S(1)}, bf16[3,128,384]{2,1,0:T(8,128)(2,1)S(1)}, u32[]{:S(2)}, u32[]{:S(2)}) collective-permute-start(bf16[3,128,384]{2,1,0:T(8,128)(2,1)S(1)} %collective-permute-done.8.refs_10_), channel_id=1, source_target_pairs={{0,1},{2,0},{4,2},{6,4},{7,6},{5,7},{3,5},{1,3},{8,9},{10,8},{12,1... | collective-permute-start | bytes 884744 | tf_op jit(solution)/shard_map/ppermute | solution.py:293
  50.7 0.4 collective-permute-start.20
  51.1 1.7 %collective-permute-start.16 = (bf16[3,128,384]{2,1,0:T(8,128)(2,1)S(1)}, bf16[3,128,384]{2,1,0:T(8,128)(2,1)S(1)}, u32[]{:S(2)}, u32[]{:S(2)}) collective-permute-start(bf16[3,128,384]{2,1,0:T(8,128)(2,1)S(1)} %collective-permute-done.15.refs_8_), channel_id=1, source_target_pairs={{0,2},{2,4},{4,6},{6,7},{7,5},{5,3},{3,1},{1,0},{8,10},{10,12},{12... | collective-permute-start | bytes 884744 | tf_op jit(solution)/shard_map/ppermute | solution.py:293
  52.8 0.3 collective-permute-start.19
  53.1 4.1 %collective-permute-done.2.refs_2_ = bf16[128,1024]{1,0:T(8,128)(2,1)S(1)} collective-permute-done((bf16[128,1024]{1,0:T(8,128)(2,1)S(1)}, bf16[128,1024]{1,0:T(8,128)(2,1)S(1)}, u32[]{:S(2)}, u32[]{:S(2)}) %collective-permute-start.2) | collective-permute-done | bytes 262176 | tf_op jit(solution)/shard_map/ppermute | solution.py:357
  57.2 8.3 %collective-permute-done.3.refs_3_ = bf16[128,1024]{1,0:T(8,128)(2,1)S(1)} collective-permute-done((bf16[128,1024]{1,0:T(8,128)(2,1)S(1)}, bf16[128,1024]{1,0:T(8,128)(2,1)S(1)}, u32[]{:S(2)}, u32[]{:S(2)}) %collective-permute-start.3) | collective-permute-done | bytes 262176 | tf_op jit(solution)/shard_map/ppermute | solution.py:357
  65.6 2.4 %shard_map.103 = (bf16[1024,512]{1,0:T(8,128)(2,1)S(1)}, f32[512,384]{1,0:T(8,128)S(1)}, f32[512,384]{1,0:T(8,128)S(1)}, f32[8,384]{1,0:T(8,128)S(1)}, bf16[512,...) custom-call(bf16[128,1024]{1,0:T(8,128)(2,1)S(1)} %get-tuple-element.36.refs_0_, ...), custom_call_target="tpu_custom_call" | custom-call | tf_op jit(solution)/shard_map/pallas_call | solution.py:319
  68.0 2.4 %shard_map.104 = (bf16[512,1152]{1,0:T(8,128)(2,1)S(1)}, bf16[64,1152]{1,0:T(8,128)(2,1)S(1)}, bf16[64,1152]{1,0:T(8,128)(2,1)S(1)}, bf16[64,1152]{1,0:T(8,128)(...) custom-call(bf16[1024,512]{1,0:T(8,128)(2,1)S(1)} %get-tuple-element.44.refs_0_.t, ...), custom_call_target="tpu_custom_call" | custom-call | tf_op jit(solution)/shard_map/pallas_call | solution.py:319
  70.5 1.6 %collective-permute-start.31 = (bf16[64,1152]{1,0:T(8,128)(2,1)S(1)}, bf16[64,1152]{1,0:T(8,128)(2,1)S(1)}, u32[]{:S(2)}, u32[]{:S(2)}) collective-permute-start(bf16[64,1152]{1,0:T(8,128)(2,1)S(1)} %get-tuple-element.63), channel_id=1, source_target_pairs={{0,1},{2,0},{4,2},{6,4},{7,6},{5,7},{3,5},{1,3},{8,9},{10,8},{12,1... | collective-permute-start | bytes 442376 | tf_op jit(solution)/shard_map/ppermute | solution.py:305
  72.1 1.0 %shard_map.105 = (bf16[64,1152]{1,0:T(8,128)(2,1)S(1)}, bf16[64,1152]{1,0:T(8,128)(2,1)S(1)}, bf16[64,1152]{1,0:T(8,128)(2,1)S(1)}, bf16[64,1152]{1,0:T(8,128)(2...) custom-call(bf16[1024,512]{1,0:T(8,128)(2,1)S(1)} %get-tuple-element, ...), custom_call_target="tpu_custom_call" | custom-call | tf_op jit(solution)/shard_map/pallas_call | solution.py:319
  73.1 0.5 collective-permute-start.28
  73.6 1.6 %collective-permute-start.25 = (bf16[64,1152]{1,0:T(8,128)(2,1)S(1)}, bf16[64,1152]{1,0:T(8,128)(2,1)S(1)}, u32[]{:S(2)}, u32[]{:S(2)}) collective-permute-start(bf16[64,1152]{1,0:T(8,128)(2,1)S(1)} %get-tuple-element.56), channel_id=1, source_target_pairs={{0,1},{2,0},{4,2},{6,4},{7,6},{5,7},{3,5},{1,3},{8,9},{10,8},{12,1... | collective-permute-start | bytes 442376 | tf_op jit(solution)/shard_map/ppermute | solution.py:305
  75.2 0.4 collective-permute-start.21
  75.6 1.1 %collective-permute-done.31 = bf16[64,1152]{1,0:T(8,128)(2,1)S(1)} collective-permute-done((bf16[64,1152]{1,0:T(8,128)(2,1)S(1)}, bf16[64,1152]{1,0:T(8,128)(2,1)S(1)}, u32[]{:S(2)}, u32[]{:S(2)}) %collective-permute-start.31) | collective-permute-done | bytes 147488 | tf_op jit(solution)/shard_map/ppermute | solution.py:305
  76.8 1.6 %collective-permute-start.32 = (bf16[64,1152]{1,0:T(8,128)(2,1)S(1)}, bf16[64,1152]{1,0:T(8,128)(2,1)S(1)}, u32[]{:S(2)}, u32[]{:S(2)}) collective-permute-start(bf16[64,1152]{1,0:T(8,128)(2,1)S(1)} %add_convert_fusion.2), channel_id=1, source_target_pairs={{0,1},{2,0},{4,2},{6,4},{7,6},{5,7},{3,5},{1,3},{8,9},{10,8},{12,1... | collective-permute-start | bytes 442376 | tf_op jit(solution)/shard_map/ppermute | solution.py:305
  78.4 1.5 %collective-permute-done.28 = bf16[64,1152]{1,0:T(8,128)(2,1)S(1)} collective-permute-done((bf16[64,1152]{1,0:T(8,128)(2,1)S(1)}, bf16[64,1152]{1,0:T(8,128)(2,1)S(1)}, u32[]{:S(2)}, u32[]{:S(2)}) %collective-permute-start.28) | collective-permute-done | bytes 147488 | tf_op jit(solution)/shard_map/ppermute | solution.py:305
  79.9 0.5 collective-permute-start.29
  80.5 1.6 %collective-permute-start.26 = (bf16[64,1152]{1,0:T(8,128)(2,1)S(1)}, bf16[64,1152]{1,0:T(8,128)(2,1)S(1)}, u32[]{:S(2)}, u32[]{:S(2)}) collective-permute-start(bf16[64,1152]{1,0:T(8,128)(2,1)S(1)} %add_convert_fusion.6), channel_id=1, source_target_pairs={{0,1},{2,0},{4,2},{6,4},{7,6},{5,7},{3,5},{1,3},{8,9},{10,8},{12,1... | collective-permute-start | bytes 442376 | tf_op jit(solution)/shard_map/ppermute | solution.py:305
  82.1 0.8 collective-permute-done.21
  83.0 0.6 collective-permute-start.22
  83.6 1.6 %collective-permute-start.33 = (bf16[64,1152]{1,0:T(8,128)(2,1)S(1)}, bf16[64,1152]{1,0:T(8,128)(2,1)S(1)}, u32[]{:S(2)}, u32[]{:S(2)}) collective-permute-start(bf16[64,1152]{1,0:T(8,128)(2,1)S(1)} %add_convert_fusion.1), channel_id=1, source_target_pairs={{0,1},{2,0},{4,2},{6,4},{7,6},{5,7},{3,5},{1,3},{8,9},{10,8},{12,1... | collective-permute-start | bytes 442376 | tf_op jit(solution)/shard_map/ppermute | solution.py:305
  85.2 1.5 %collective-permute-done.29 = bf16[64,1152]{1,0:T(8,128)(2,1)S(1)} collective-permute-done((bf16[64,1152]{1,0:T(8,128)(2,1)S(1)}, bf16[64,1152]{1,0:T(8,128)(2,1)S(1)}, u32[]{:S(2)}, u32[]{:S(2)}) %collective-permute-start.29) | collective-permute-done | bytes 147488 | tf_op jit(solution)/shard_map/ppermute | solution.py:305
  86.8 0.5 collective-permute-start.30
  87.3 1.6 %collective-permute-start.27 = (bf16[64,1152]{1,0:T(8,128)(2,1)S(1)}, bf16[64,1152]{1,0:T(8,128)(2,1)S(1)}, u32[]{:S(2)}, u32[]{:S(2)}) collective-permute-start(bf16[64,1152]{1,0:T(8,128)(2,1)S(1)} %add_convert_fusion.5), channel_id=1, source_target_pairs={{0,1},{2,0},{4,2},{6,4},{7,6},{5,7},{3,5},{1,3},{8,9},{10,8},{12,1... | collective-permute-start | bytes 442376 | tf_op jit(solution)/shard_map/ppermute | solution.py:305
  88.9 0.9 collective-permute-done.22
  89.9 0.4 collective-permute-start.23
  90.3 0.1 collective-permute-done.33
  90.5 1.6 %collective-permute-start.34 = (bf16[64,1152]{1,0:T(8,128)(2,1)S(1)}, bf16[64,1152]{1,0:T(8,128)(2,1)S(1)}, u32[]{:S(2)}, u32[]{:S(2)}) collective-permute-start(bf16[64,1152]{1,0:T(8,128)(2,1)S(1)} %add_convert_fusion), channel_id=1, source_target_pairs={{0,1},{2,0},{4,2},{6,4},{7,6},{5,7},{3,5},{1,3},{8,9},{10,8},{12,1... | collective-permute-start | bytes 442376 | tf_op jit(solution)/shard_map/ppermute | solution.py:305
  92.1 3.0 %collective-permute-done.23 = bf16[64,1152]{1,0:T(8,128)(2,1)S(1)} collective-permute-done((bf16[64,1152]{1,0:T(8,128)(2,1)S(1)}, bf16[64,1152]{1,0:T(8,128)(2,1)S(1)}, u32[]{:S(2)}, u32[]{:S(2)}) %collective-permute-start.23) | collective-permute-done | bytes 147488 | tf_op jit(solution)/shard_map/ppermute | solution.py:305
  95.2 0.4 collective-permute-start.24
  95.6 0.1 collective-permute-done.34.refs_5_
  95.6 4.7 %collective-permute-done.24.refs_1_ = bf16[64,1152]{1,0:T(8,128)(2,1)S(1)} collective-permute-done((bf16[64,1152]{1,0:T(8,128)(2,1)S(1)}, bf16[64,1152]{1,0:T(8,128)(2,1)S(1)}, u32[]{:S(2)}, u32[]{:S(2)}) %collective-permute-start.24) | collective-permute-done | bytes 147488 | tf_op jit(solution)/shard_map/ppermute | solution.py:305
  100.4 0.9 shard_map.106
  (51 shorter events, 0.5 us)
Async XLA Ops:
  0.0 9.9 %slice-start.1 = ((bf16[512,512]{1,0:T(8,128)(2,1)}), bf16[256,512]{1,0:T(8,128)(2,1)S(1)}, s32[]{:S(2)}) async-start(bf16[512,512]{1,0:T(8,128)(2,1)} %k_ref.3), calls=%async_computation.1 | async-start | bytes 524288 | tf_op jit(solution)/shard_map/slice | solution.py:341
  0.0 9.9 %slice-start = ((bf16[512,512]{1,0:T(8,128)(2,1)}), bf16[256,512]{1,0:T(8,128)(2,1)S(1)}, s32[]{:S(2)}) async-start(bf16[512,512]{1,0:T(8,128)(2,1)} %v_ref.3), calls=%async_computation | async-start | bytes 524288 | tf_op jit(solution)/shard_map/slice | solution.py:341
  0.0 1.3 %copy-start.5 = (bf16[512,1024]{1,0:T(8,128)(2,1)S(1)}, bf16[512,1024]{1,0:T(8,128)(2,1)}, u32[]{:S(2)}) copy-start(bf16[512,1024]{1,0:T(8,128)(2,1)} %param.19) | copy-start | bytes 3145732
  1.3 0.7 copy-start.8
  1.9 39.4 %copy-start.2 = (bf16[512,512]{1,0:T(8,128)(2,1)S(1)}, bf16[512,512]{1,0:T(8,128)(2,1)}, u32[]{:S(2)}) copy-start(bf16[512,512]{1,0:T(8,128)(2,1)} %v_ref.3) | copy-start | bytes 1572868
  2.7 38.6 %copy-start = (bf16[512,1024]{1,0:T(8,128)(2,1)S(1)}, bf16[512,1024]{1,0:T(8,128)(2,1)}, u32[]{:S(2)}) copy-start(bf16[512,1024]{1,0:T(8,128)(2,1)} %r_ref.3) | copy-start | bytes 3145732
  2.7 38.6 %copy-start.1 = (bf16[512,1024]{1,0:T(8,128)(2,1)S(1)}, bf16[512,1024]{1,0:T(8,128)(2,1)}, u32[]{:S(2)}) copy-start(bf16[512,1024]{1,0:T(8,128)(2,1)} %wo_ref.3) | copy-start | bytes 3145732
  2.7 6.7 %collective-permute-start.4 = (bf16[144,1024]{1,0:T(8,128)(2,1)S(1)}, bf16[144,1024]{1,0:T(8,128)(2,1)S(1)}, u32[]{:S(2)}, u32[]{:S(2)}) collective-permute-start(bf16[144,1024]{1,0:T(8,128)(2,1)S(1)} %get-tuple-element.41), channel_id=1, source_target_pairs={{0,8},{8,0},{16,24},{24,16},{1,9},{9,1},{17,25},{25,17},{2,10},{10... | collective-permute-start | bytes 884744 | tf_op jit(solution)/shard_map/ppermute | solution.py:357
  3.3 10.2 %collective-permute-start.5 = (bf16[144,1024]{1,0:T(8,128)(2,1)S(1)}, bf16[144,1024]{1,0:T(8,128)(2,1)S(1)}, u32[]{:S(2)}, u32[]{:S(2)}) collective-permute-start(bf16[144,1024]{1,0:T(8,128)(2,1)S(1)} %get-tuple-element.42), channel_id=1, source_target_pairs={{0,16},{8,24},{16,0},{24,8},{1,17},{9,25},{17,1},{25,9},{2,18},{10... | collective-permute-start | bytes 884744 | tf_op jit(solution)/shard_map/ppermute | solution.py:357
  5.9 17.3 %collective-permute-start.11 = (bf16[3,384,128]{2,1,0:T(8,128)(2,1)}, bf16[3,384,128]{2,1,0:T(8,128)(2,1)S(1)}, u32[]{:S(2)}, u32[]{:S(2)}) collective-permute-start(bf16[3,384,128]{2,1,0:T(8,128)(2,1)} %refs_13_.1), channel_id=1, source_target_pairs={{0,1},{2,0},{4,2},{6,4},{7,6},{5,7},{3,5},{1,3},{8,9},{10,8},{12,1... | collective-permute-start | bytes 884744 | tf_op jit(solution)/shard_map/ppermute | solution.py:293
  7.4 17.3 %collective-permute-start.13 = (bf16[3,384,128]{2,1,0:T(8,128)(2,1)}, bf16[3,384,128]{2,1,0:T(8,128)(2,1)S(1)}, u32[]{:S(2)}, u32[]{:S(2)}) collective-permute-start(bf16[3,384,128]{2,1,0:T(8,128)(2,1)} %refs_13_.1), channel_id=1, source_target_pairs={{0,2},{2,4},{4,6},{6,7},{7,5},{5,3},{3,1},{1,0},{8,10},{10,12},{12... | collective-permute-start | bytes 884744 | tf_op jit(solution)/shard_map/ppermute | solution.py:293
  7.9 14.8 %collective-permute-start.9 = (bf16[3,128,384]{2,1,0:T(8,128)(2,1)}, bf16[3,128,384]{2,1,0:T(8,128)(2,1)S(1)}, u32[]{:S(2)}, u32[]{:S(2)}) collective-permute-start(bf16[3,128,384]{2,1,0:T(8,128)(2,1)} %refs_8_.1), channel_id=1, source_target_pairs={{0,2},{2,4},{4,6},{6,7},{7,5},{5,3},{3,1},{1,0},{8,10},{10,12},{12... | collective-permute-start | bytes 884744 | tf_op jit(solution)/shard_map/ppermute | solution.py:293
  9.5 15.2 %collective-permute-start.7 = (bf16[3,128,384]{2,1,0:T(8,128)(2,1)}, bf16[3,128,384]{2,1,0:T(8,128)(2,1)S(1)}, u32[]{:S(2)}, u32[]{:S(2)}) collective-permute-start(bf16[3,128,384]{2,1,0:T(8,128)(2,1)} %refs_8_.1), channel_id=1, source_target_pairs={{0,1},{2,0},{4,2},{6,4},{7,6},{5,7},{3,5},{1,3},{8,9},{10,8},{12,1... | collective-permute-start | bytes 884744 | tf_op jit(solution)/shard_map/ppermute | solution.py:293
  13.5 19.1 %collective-permute-start = (bf16[256,1024]{1,0:T(8,128)(2,1)S(1)}, bf16[256,1024]{1,0:T(8,128)(2,1)S(1)}, u32[]{:S(2)}, u32[]{:S(2)}) collective-permute-start(bf16[256,1024]{1,0:T(8,128)(2,1)S(1)} %pad_maximum_fusion), channel_id=1, source_target_pairs={{0,1},{1,2},{2,3},{3,4},{4,5},{5,6},{6,7},{8,9},{9,10},{10,11},{11... | collective-permute-start | bytes 1572872 | tf_op jit(solution)/shard_map/ppermute | solution.py:342
  22.7 12.3 %collective-permute-start.10 = (bf16[3,128,384]{2,1,0:T(8,128)(2,1)S(1)}, bf16[3,128,384]{2,1,0:T(8,128)(2,1)S(1)}, u32[]{:S(2)}, u32[]{:S(2)}) collective-permute-start(bf16[3,128,384]{2,1,0:T(8,128)(2,1)S(1)} %collective-permute-done.9.refs_12_), channel_id=1, source_target_pairs={{0,2},{2,4},{4,6},{6,7},{7,5},{5,3},{3,1},{1,0},{8,10},{10,12},{12... | collective-permute-start | bytes 884744 | tf_op jit(solution)/shard_map/ppermute | solution.py:293
  23.2 15.6 %collective-permute-start.12 = (bf16[3,384,128]{2,1,0:T(8,128)(2,1)S(1)}, bf16[3,384,128]{2,1,0:T(8,128)(2,1)S(1)}, u32[]{:S(2)}, u32[]{:S(2)}) collective-permute-start(bf16[3,384,128]{2,1,0:T(8,128)(2,1)S(1)} %collective-permute-done.11.refs_14_), channel_id=1, source_target_pairs={{0,1},{2,0},{4,2},{6,4},{7,6},{5,7},{3,5},{1,3},{8,9},{10,8},{12,1... | collective-permute-start | bytes 884744 | tf_op jit(solution)/shard_map/ppermute | solution.py:293
  24.7 20.9 %copy-start.9 = (s32[8]{0:T(128)S(1)}, s32[8]{0:T(128)}, u32[]{:S(2)}) copy-start(s32[8]{0:T(128)} %lang_ref.3) | copy-start | bytes 100
  24.7 23.7 %collective-permute-start.6 = (bf16[144,1024]{1,0:T(8,128)(2,1)S(1)}, bf16[144,1024]{1,0:T(8,128)(2,1)S(1)}, u32[]{:S(2)}, u32[]{:S(2)}) collective-permute-start(bf16[144,1024]{1,0:T(8,128)(2,1)S(1)} %get-tuple-element.43), channel_id=1, source_target_pairs={{0,24},{8,16},{16,8},{24,0},{1,25},{9,17},{17,9},{25,1},{2,26},{10... | collective-permute-start | bytes 884744 | tf_op jit(solution)/shard_map/ppermute | solution.py:357
  24.7 23.8 %collective-permute-start.14 = (bf16[3,384,128]{2,1,0:T(8,128)(2,1)S(1)}, bf16[3,384,128]{2,1,0:T(8,128)(2,1)S(1)}, u32[]{:S(2)}, u32[]{:S(2)}) collective-permute-start(bf16[3,384,128]{2,1,0:T(8,128)(2,1)S(1)} %collective-permute-done.13.refs_17_), channel_id=1, source_target_pairs={{0,2},{2,4},{4,6},{6,7},{7,5},{5,3},{3,1},{1,0},{8,10},{10,12},{12... | collective-permute-start | bytes 884744 | tf_op jit(solution)/shard_map/ppermute | solution.py:293
  32.5 16.6 %collective-permute-start.8 = (bf16[3,128,384]{2,1,0:T(8,128)(2,1)S(1)}, bf16[3,128,384]{2,1,0:T(8,128)(2,1)S(1)}, u32[]{:S(2)}, u32[]{:S(2)}) collective-permute-start(bf16[3,128,384]{2,1,0:T(8,128)(2,1)S(1)} %collective-permute-done.7.refs_9_), channel_id=1, source_target_pairs={{0,1},{2,0},{4,2},{6,4},{7,6},{5,7},{3,5},{1,3},{8,9},{10,8},{12,1... | collective-permute-start | bytes 884744 | tf_op jit(solution)/shard_map/ppermute | solution.py:293
  35.0 16.1 %collective-permute-start.15 = (bf16[3,128,384]{2,1,0:T(8,128)(2,1)S(1)}, bf16[3,128,384]{2,1,0:T(8,128)(2,1)S(1)}, u32[]{:S(2)}, u32[]{:S(2)}) collective-permute-start(bf16[3,128,384]{2,1,0:T(8,128)(2,1)S(1)} %collective-permute-done.10.refs_11_), channel_id=1, source_target_pairs={{0,2},{2,4},{4,6},{6,7},{7,5},{5,3},{3,1},{1,0},{8,10},{10,12},{12... | collective-permute-start | bytes 884744 | tf_op jit(solution)/shard_map/ppermute | solution.py:293
  38.8 14.0 %collective-permute-start.18 = (bf16[3,384,128]{2,1,0:T(8,128)(2,1)S(1)}, bf16[3,384,128]{2,1,0:T(8,128)(2,1)S(1)}, u32[]{:S(2)}, u32[]{:S(2)}) collective-permute-start(bf16[3,384,128]{2,1,0:T(8,128)(2,1)S(1)} %collective-permute-done.12.refs_15_), channel_id=1, source_target_pairs={{0,1},{2,0},{4,2},{6,4},{7,6},{5,7},{3,5},{1,3},{8,9},{10,8},{12,1... | collective-permute-start | bytes 884744 | tf_op jit(solution)/shard_map/ppermute | solution.py:293
  41.3 1.0 %copy-start.3 = (bf16[512,512]{1,0:T(8,128)(2,1)S(1)}, bf16[512,512]{1,0:T(8,128)(2,1)}, u32[]{:S(2)}) copy-start(bf16[512,512]{1,0:T(8,128)(2,1)} %k_ref.3) | copy-start | bytes 1572868
  42.4 1.0 %copy-start.4 = (bf16[512,512]{1,0:T(8,128)(2,1)S(1)}, bf16[512,512]{1,0:T(8,128)(2,1)}, u32[]{:S(2)}) copy-start(bf16[512,512]{1,0:T(8,128)(2,1)} %q_ref.3) | copy-start | bytes 1572868
  45.6 11.6 %copy-start.10 = (bf16[3,384]{1,0:T(4,128)(2,1)S(1)}, bf16[3,384]{1,0:T(4,128)(2,1)}, u32[]{:S(2)}) copy-start(bf16[3,384]{1,0:T(4,128)(2,1)} %param.18) | copy-start | bytes 6916
  45.6 20.0 %copy-start.6 = (bf16[3,128,384]{2,1,0:T(8,128)(2,1)S(1)}, bf16[3,128,384]{2,1,0:T(8,128)(2,1)}, u32[]{:S(2)}) copy-start(bf16[3,128,384]{2,1,0:T(8,128)(2,1)} %refs_8_.1) | copy-start | bytes 884740
  45.6 20.0 %copy-start.7 = (bf16[3,384,128]{2,1,0:T(8,128)(2,1)S(1)}, bf16[3,384,128]{2,1,0:T(8,128)(2,1)}, u32[]{:S(2)}) copy-start(bf16[3,384,128]{2,1,0:T(8,128)(2,1)} %refs_13_.1) | copy-start | bytes 884740
  48.4 2.2 %collective-permute-start.1 = (bf16[128,1024]{1,0:T(8,128)(2,1)S(1)}, bf16[128,1024]{1,0:T(8,128)(2,1)S(1)}, u32[]{:S(2)}, u32[]{:S(2)}) collective-permute-start(bf16[128,1024]{1,0:T(8,128)(2,1)S(1)} %get-tuple-element.37), channel_id=1, source_target_pairs={{0,8},{8,0},{16,24},{24,16},{1,9},{9,1},{17,25},{25,17},{2,10},{10... | collective-permute-start | bytes 786440 | tf_op jit(solution)/shard_map/ppermute | solution.py:357
  48.5 8.7 %collective-permute-start.2 = (bf16[128,1024]{1,0:T(8,128)(2,1)S(1)}, bf16[128,1024]{1,0:T(8,128)(2,1)S(1)}, u32[]{:S(2)}, u32[]{:S(2)}) collective-permute-start(bf16[128,1024]{1,0:T(8,128)(2,1)S(1)} %get-tuple-element.38), channel_id=1, source_target_pairs={{0,16},{8,24},{16,0},{24,8},{1,17},{9,25},{17,1},{25,9},{2,18},{10... | collective-permute-start | bytes 786440 | tf_op jit(solution)/shard_map/ppermute | solution.py:357
  49.1 18.9 %collective-permute-start.17 = (bf16[3,128,384]{2,1,0:T(8,128)(2,1)S(1)}, bf16[3,128,384]{2,1,0:T(8,128)(2,1)S(1)}, u32[]{:S(2)}, u32[]{:S(2)}) collective-permute-start(bf16[3,128,384]{2,1,0:T(8,128)(2,1)S(1)} %collective-permute-done.8.refs_10_), channel_id=1, source_target_pairs={{0,1},{2,0},{4,2},{6,4},{7,6},{5,7},{3,5},{1,3},{8,9},{10,8},{12,1... | collective-permute-start | bytes 884744 | tf_op jit(solution)/shard_map/ppermute | solution.py:293
  50.7 17.3 %collective-permute-start.20 = (bf16[3,384,128]{2,1,0:T(8,128)(2,1)S(1)}, bf16[3,384,128]{2,1,0:T(8,128)(2,1)S(1)}, u32[]{:S(2)}, u32[]{:S(2)}) collective-permute-start(bf16[3,384,128]{2,1,0:T(8,128)(2,1)S(1)} %collective-permute-done.14.refs_16_), channel_id=1, source_target_pairs={{0,2},{2,4},{4,6},{6,7},{7,5},{5,3},{3,1},{1,0},{8,10},{10,12},{12... | collective-permute-start | bytes 884744 | tf_op jit(solution)/shard_map/ppermute | solution.py:293
  51.1 16.9 %collective-permute-start.16 = (bf16[3,128,384]{2,1,0:T(8,128)(2,1)S(1)}, bf16[3,128,384]{2,1,0:T(8,128)(2,1)S(1)}, u32[]{:S(2)}, u32[]{:S(2)}) collective-permute-start(bf16[3,128,384]{2,1,0:T(8,128)(2,1)S(1)} %collective-permute-done.15.refs_8_), channel_id=1, source_target_pairs={{0,2},{2,4},{4,6},{6,7},{7,5},{5,3},{3,1},{1,0},{8,10},{10,12},{12... | collective-permute-start | bytes 884744 | tf_op jit(solution)/shard_map/ppermute | solution.py:293
  52.8 15.2 %collective-permute-start.19 = (bf16[3,384,128]{2,1,0:T(8,128)(2,1)S(1)}, bf16[3,384,128]{2,1,0:T(8,128)(2,1)S(1)}, u32[]{:S(2)}, u32[]{:S(2)}) collective-permute-start(bf16[3,384,128]{2,1,0:T(8,128)(2,1)S(1)} %collective-permute-done.18.refs_10_), channel_id=1, source_target_pairs={{0,1},{2,0},{4,2},{6,4},{7,6},{5,7},{3,5},{1,3},{8,9},{10,8},{12,1... | collective-permute-start | bytes 884744 | tf_op jit(solution)/shard_map/ppermute | solution.py:293
  57.2 8.4 %collective-permute-start.3 = (bf16[128,1024]{1,0:T(8,128)(2,1)S(1)}, bf16[128,1024]{1,0:T(8,128)(2,1)S(1)}, u32[]{:S(2)}, u32[]{:S(2)}) collective-permute-start(bf16[128,1024]{1,0:T(8,128)(2,1)S(1)} %get-tuple-element.39), channel_id=1, source_target_pairs={{0,24},{8,16},{16,8},{24,0},{1,25},{9,17},{17,9},{25,1},{2,26},{10... | collective-permute-start | bytes 786440 | tf_op jit(solution)/shard_map/ppermute | solution.py:357
  70.5 6.3 %collective-permute-start.31 = (bf16[64,1152]{1,0:T(8,128)(2,1)S(1)}, bf16[64,1152]{1,0:T(8,128)(2,1)S(1)}, u32[]{:S(2)}, u32[]{:S(2)}) collective-permute-start(bf16[64,1152]{1,0:T(8,128)(2,1)S(1)} %get-tuple-element.63), channel_id=1, source_target_pairs={{0,1},{2,0},{4,2},{6,4},{7,6},{5,7},{3,5},{1,3},{8,9},{10,8},{12,1... | collective-permute-start | bytes 442376 | tf_op jit(solution)/shard_map/ppermute | solution.py:305
  73.1 6.8 %collective-permute-start.28 = (bf16[64,1152]{1,0:T(8,128)(2,1)S(1)}, bf16[64,1152]{1,0:T(8,128)(2,1)S(1)}, u32[]{:S(2)}, u32[]{:S(2)}) collective-permute-start(bf16[64,1152]{1,0:T(8,128)(2,1)S(1)} %get-tuple-element.60), channel_id=1, source_target_pairs={{0,2},{2,4},{4,6},{6,7},{7,5},{5,3},{3,1},{1,0},{8,10},{10,12},{12... | collective-permute-start | bytes 442376 | tf_op jit(solution)/shard_map/ppermute | solution.py:305
  73.6 6.8 %collective-permute-start.25 = (bf16[64,1152]{1,0:T(8,128)(2,1)S(1)}, bf16[64,1152]{1,0:T(8,128)(2,1)S(1)}, u32[]{:S(2)}, u32[]{:S(2)}) collective-permute-start(bf16[64,1152]{1,0:T(8,128)(2,1)S(1)} %get-tuple-element.56), channel_id=1, source_target_pairs={{0,1},{2,0},{4,2},{6,4},{7,6},{5,7},{3,5},{1,3},{8,9},{10,8},{12,1... | collective-permute-start | bytes 442376 | tf_op jit(solution)/shard_map/ppermute | solution.py:305
  75.2 7.7 %collective-permute-start.21 = (bf16[64,1152]{1,0:T(8,128)(2,1)S(1)}, bf16[64,1152]{1,0:T(8,128)(2,1)S(1)}, u32[]{:S(2)}, u32[]{:S(2)}) collective-permute-start(bf16[64,1152]{1,0:T(8,128)(2,1)S(1)} %get-tuple-element.52), channel_id=1, source_target_pairs={{0,2},{2,4},{4,6},{6,7},{7,5},{5,3},{3,1},{1,0},{8,10},{10,12},{12... | collective-permute-start | bytes 442376 | tf_op jit(solution)/shard_map/ppermute | solution.py:305
  76.8 6.8 %collective-permute-start.32 = (bf16[64,1152]{1,0:T(8,128)(2,1)S(1)}, bf16[64,1152]{1,0:T(8,128)(2,1)S(1)}, u32[]{:S(2)}, u32[]{:S(2)}) collective-permute-start(bf16[64,1152]{1,0:T(8,128)(2,1)S(1)} %add_convert_fusion.2), channel_id=1, source_target_pairs={{0,1},{2,0},{4,2},{6,4},{7,6},{5,7},{3,5},{1,3},{8,9},{10,8},{12,1... | collective-permute-start | bytes 442376 | tf_op jit(solution)/shard_map/ppermute | solution.py:305
  79.9 6.8 %collective-permute-start.29 = (bf16[64,1152]{1,0:T(8,128)(2,1)S(1)}, bf16[64,1152]{1,0:T(8,128)(2,1)S(1)}, u32[]{:S(2)}, u32[]{:S(2)}) collective-permute-start(bf16[64,1152]{1,0:T(8,128)(2,1)S(1)} %add_convert_fusion.4), channel_id=1, source_target_pairs={{0,2},{2,4},{4,6},{6,7},{7,5},{5,3},{3,1},{1,0},{8,10},{10,12},{12... | collective-permute-start | bytes 442376 | tf_op jit(solution)/shard_map/ppermute | solution.py:305
  80.5 6.8 %collective-permute-start.26 = (bf16[64,1152]{1,0:T(8,128)(2,1)S(1)}, bf16[64,1152]{1,0:T(8,128)(2,1)S(1)}, u32[]{:S(2)}, u32[]{:S(2)}) collective-permute-start(bf16[64,1152]{1,0:T(8,128)(2,1)S(1)} %add_convert_fusion.6), channel_id=1, source_target_pairs={{0,1},{2,0},{4,2},{6,4},{7,6},{5,7},{3,5},{1,3},{8,9},{10,8},{12,1... | collective-permute-start | bytes 442376 | tf_op jit(solution)/shard_map/ppermute | solution.py:305
  83.0 6.9 %collective-permute-start.22 = (bf16[64,1152]{1,0:T(8,128)(2,1)S(1)}, bf16[64,1152]{1,0:T(8,128)(2,1)S(1)}, u32[]{:S(2)}, u32[]{:S(2)}) collective-permute-start(bf16[64,1152]{1,0:T(8,128)(2,1)S(1)} %add_convert_fusion.9), channel_id=1, source_target_pairs={{0,2},{2,4},{4,6},{6,7},{7,5},{5,3},{3,1},{1,0},{8,10},{10,12},{12... | collective-permute-start | bytes 442376 | tf_op jit(solution)/shard_map/ppermute | solution.py:305
  83.6 6.8 %collective-permute-start.33 = (bf16[64,1152]{1,0:T(8,128)(2,1)S(1)}, bf16[64,1152]{1,0:T(8,128)(2,1)S(1)}, u32[]{:S(2)}, u32[]{:S(2)}) collective-permute-start(bf16[64,1152]{1,0:T(8,128)(2,1)S(1)} %add_convert_fusion.1), channel_id=1, source_target_pairs={{0,1},{2,0},{4,2},{6,4},{7,6},{5,7},{3,5},{1,3},{8,9},{10,8},{12,1... | collective-permute-start | bytes 442376 | tf_op jit(solution)/shard_map/ppermute | solution.py:305
  86.8 8.8 %collective-permute-start.30 = (bf16[64,1152]{1,0:T(8,128)(2,1)S(1)}, bf16[64,1152]{1,0:T(8,128)(2,1)S(1)}, u32[]{:S(2)}, u32[]{:S(2)}) collective-permute-start(bf16[64,1152]{1,0:T(8,128)(2,1)S(1)} %add_convert_fusion.3), channel_id=1, source_target_pairs={{0,2},{2,4},{4,6},{6,7},{7,5},{5,3},{3,1},{1,0},{8,10},{10,12},{12... | collective-permute-start | bytes 442376 | tf_op jit(solution)/shard_map/ppermute | solution.py:305
  87.3 8.3 %collective-permute-start.27 = (bf16[64,1152]{1,0:T(8,128)(2,1)S(1)}, bf16[64,1152]{1,0:T(8,128)(2,1)S(1)}, u32[]{:S(2)}, u32[]{:S(2)}) collective-permute-start(bf16[64,1152]{1,0:T(8,128)(2,1)S(1)} %add_convert_fusion.5), channel_id=1, source_target_pairs={{0,1},{2,0},{4,2},{6,4},{7,6},{5,7},{3,5},{1,3},{8,9},{10,8},{12,1... | collective-permute-start | bytes 442376 | tf_op jit(solution)/shard_map/ppermute | solution.py:305
  89.9 5.2 %collective-permute-start.23 = (bf16[64,1152]{1,0:T(8,128)(2,1)S(1)}, bf16[64,1152]{1,0:T(8,128)(2,1)S(1)}, u32[]{:S(2)}, u32[]{:S(2)}) collective-permute-start(bf16[64,1152]{1,0:T(8,128)(2,1)S(1)} %add_convert_fusion.8), channel_id=1, source_target_pairs={{0,2},{2,4},{4,6},{6,7},{7,5},{5,3},{3,1},{1,0},{8,10},{10,12},{12... | collective-permute-start | bytes 442376 | tf_op jit(solution)/shard_map/ppermute | solution.py:305
  90.5 5.2 %collective-permute-start.34 = (bf16[64,1152]{1,0:T(8,128)(2,1)S(1)}, bf16[64,1152]{1,0:T(8,128)(2,1)S(1)}, u32[]{:S(2)}, u32[]{:S(2)}) collective-permute-start(bf16[64,1152]{1,0:T(8,128)(2,1)S(1)} %add_convert_fusion), channel_id=1, source_target_pairs={{0,1},{2,0},{4,2},{6,4},{7,6},{5,7},{3,5},{1,3},{8,9},{10,8},{12,1... | collective-permute-start | bytes 442376 | tf_op jit(solution)/shard_map/ppermute | solution.py:305
  95.2 5.2 %collective-permute-start.24 = (bf16[64,1152]{1,0:T(8,128)(2,1)S(1)}, bf16[64,1152]{1,0:T(8,128)(2,1)S(1)}, u32[]{:S(2)}, u32[]{:S(2)}) collective-permute-start(bf16[64,1152]{1,0:T(8,128)(2,1)S(1)} %add_convert_fusion.7), channel_id=1, source_target_pairs={{0,2},{2,4},{4,6},{6,7},{7,5},{5,3},{3,1},{1,0},{8,10},{10,12},{12... | collective-permute-start | bytes 442376 | tf_op jit(solution)/shard_map/ppermute | solution.py:305
